TPU v7x, 768 devices: a whole 4x8x12 slice. The times are simulated.
768 devices in a mesh: gx: 32 (over x, y_hi, core), gy: 24 (over z, y_lo).
Axes of the slice: x: 4, y: 8 (y_hi: 4, y_lo: 2; y = y_hi * 2 + y_lo), z: 12, core: 2. Of those that a mesh axis runs over, the one named last changes fastest.
Arguments:
- fields: float32 [3, 8, 3072, 3072], P(None, None, 'gx', 'gy'), may hold values from -6 to 6
- terrain: int32 [3072, 3072], P('gx', 'gy'), may hold values from 0 to 2999
- parent_columns: bfloat16 [3, 60, 294912], P(None, None, ('gx', 'gy')), may hold values from -6 to 6
- record_tile: int32 [294912, 1], P(('gx', 'gy')), may hold values from 0 to 31; in each aligned block of 384 rows (0 to 383, 384 to 767, ...) at most 24 rows name the same one
- record_cells: int32 [294912, 4], P(('gx', 'gy')), may hold values from 0 to 191
- record_weights: bfloat16 [294912, 4], P(('gx', 'gy')), may hold values from 0.049804688 to 1
Outputs:
- updated_state: float32 [3, 8, 3072, 3072], P(None, None, 'gx', 'gy')
- nudge_coeffs: float32 [3, 8, 32, 32], replicated
Inputs may be any that keep to these rules, and one draw needn't show every extreme that they name: `record_tile`: at most 24 of the 384 records of one device name the same tile index, and some device names one tile index exactly 24 times.
All inputs are finite; a program needn't handle non-finite values.
Results may differ from a plain program's by a relative error of at most 0.0003.
Values may be sent and summed in bfloat16 or wider, within the bound.
No kernel may reach another device: no remote copies, remote signals or barrier semaphores. Data moves between devices by JAX's collectives and lax.ppermute only.
A program may use at most 64 MiB of HBM per device.

v0:
```python
import math

import jax
import jax.numpy as jnp
from jax import lax
from jax.sharding import PartitionSpec as P

KW = 32
RATIO = 8


top_height = 12000.0


def padded_2(cells, sides, width):
    for axis, dim in sides:
        count = lax.axis_size(axis)
        ends = count - 1
        head = lax.slice_in_dim(cells, 0, width, axis=dim)
        tail = lax.slice_in_dim(cells, cells.shape[dim] - width, cells.shape[dim], axis=dim)
        cells = jnp.concatenate(
            [
                lax.ppermute(tail, axis, [(i, (i + 1) % count) for i in range(ends)]),
                cells,
                lax.ppermute(head, axis, [((i + 1) % count, i) for i in range(ends)]),
            ],
            axis=dim,
        )
    return cells


def octant_table():
    half_root = math.sqrt(0.5)
    cos_table = jnp.array(
        [1.0, half_root, 0.0, -half_root, -1.0, -half_root, 0.0, half_root, 1.0], jnp.float32
    )
    sin_table = jnp.array(
        [0.0, half_root, 1.0, half_root, 0.0, -half_root, -1.0, -half_root, 0.0], jnp.float32
    )
    return (cos_table, sin_table)


def wave_basis(positions, length, modes):
    half = modes // 2
    orders = jnp.arange(modes, dtype=jnp.int32)
    wave_number = jnp.where(orders < half, orders, orders - half + 1)
    phase_index = wave_number[:, None] * positions[None, :] % length
    octant = (8 * phase_index + length // 2) // length
    remainder = 8 * phase_index - octant * length
    small_angle = 2.0 * math.pi / (8 * length) * remainder.astype(jnp.float32)
    cos_table, sin_table = octant_table()
    octant_hot = (octant[:, :, None] == jnp.arange(9, dtype=jnp.int32)[None, None, :]).astype(
        jnp.float32
    )
    cos_octant = jnp.sum(octant_hot * cos_table, axis=2)
    sin_octant = jnp.sum(octant_hot * sin_table, axis=2)
    cos_small = jnp.cos(small_angle)
    sin_small = jnp.sin(small_angle)
    cos_value = cos_octant * cos_small - sin_octant * sin_small
    sin_value = sin_octant * cos_small + cos_octant * sin_small
    wave_rows = jnp.where((orders < half)[:, None], cos_value, sin_value) * math.sqrt(2.0)
    return jnp.where((orders == 0)[:, None], jnp.ones_like(wave_rows), wave_rows)


def level_weights(heights, levels, parent_levels):
    spacing = (top_height - heights) / levels
    nest_height = (
        heights[None, :] + (jnp.arange(levels, dtype=jnp.float32)[:, None] + 0.5) * spacing[None, :]
    )
    parent_height = (jnp.arange(parent_levels, dtype=jnp.float32) + 0.5) * (
        top_height / parent_levels
    )
    hat_weights = jnp.maximum(
        0.0,
        1.0
        - jnp.abs(nest_height[:, None, :] - parent_height[None, :, None]) / spacing[None, None, :],
    )
    return hat_weights / jnp.sum(hat_weights, axis=1, keepdims=True)


def project(values, basis_x, basis_y):
    along_x = jnp.einsum("mx,vkxy->vkmy", basis_x, values, precision=lax.Precision.HIGHEST)
    return jnp.einsum("vkmy,ny->vkmn", along_x, basis_y, precision=lax.Precision.HIGHEST)


def expand(coeffs, basis_x, basis_y):
    along_y = jnp.einsum("vkmn,ny->vkmy", coeffs, basis_y, precision=lax.Precision.HIGHEST)
    return jnp.einsum("mx,vkmy->vkxy", basis_x, along_y, precision=lax.Precision.HIGHEST)


def advance(padded, values, wind_x, wind_y, inv_metric, low_modes):
    east_side = padded[:, :, 2:, 1:-1]
    west_side = padded[:, :, :-2, 1:-1]
    north_side = padded[:, :, 1:-1, 2:]
    south_side = padded[:, :, 1:-1, :-2]
    transport = 0.5 * (wind_x * (east_side - west_side) + wind_y * (north_side - south_side))
    diffusion = east_side + west_side + north_side + south_side - 4.0 * values
    level_above = jnp.concatenate([values[:, 1:], values[:, -1:]], axis=1)
    level_below = jnp.concatenate([values[:, :1], values[:, :-1]], axis=1)
    mixing = (level_above - 2.0 * values + level_below) * inv_metric
    return values - 0.1 * transport + 0.1 * diffusion + 0.1 * mixing - 4.0 * low_modes


def per_device(fields, terrain, parent_columns, record_tile, record_cells, record_weights):
    tiles_x = lax.axis_size("gx")
    tiles_y = lax.axis_size("gy")
    variables = fields.shape[0]
    levels = fields.shape[1]
    cells_x = fields.shape[2]
    cells_y = fields.shape[3]
    total_x = cells_x * tiles_x
    total_y = cells_y * tiles_y
    records_here = record_tile.shape[0]
    coarse_x = cells_x // RATIO
    coarse_y = cells_y // RATIO
    coarse_count = coarse_x * coarse_y
    scale = 1.0 / math.sqrt(total_x * total_y)
    cols_x = lax.axis_index("gx") * cells_x + jnp.arange(cells_x, dtype=jnp.int32)
    cols_y = lax.axis_index("gy") * cells_y + jnp.arange(cells_y, dtype=jnp.int32)
    basis_x = wave_basis(cols_x, total_x, KW)
    basis_y = wave_basis(cols_y, total_y, KW)
    capacity = 2 * records_here // tiles_x
    count_of_slots = tiles_x * capacity
    target_position = record_tile[:, 0]
    tile_hot = (target_position[:, None] == jnp.arange(tiles_x, dtype=jnp.int32)[None, :]).astype(
        jnp.int32
    )
    earlier = jnp.cumsum(tile_hot, axis=0) - tile_hot
    rank_in_tile = jnp.sum(earlier * tile_hot, axis=1)
    slot_index = target_position * capacity + rank_in_tile
    scattered_values = (
        slot_index[:, None] == jnp.arange(count_of_slots, dtype=jnp.int32)[None, :]
    ).astype(jnp.int32)
    source_row = jnp.sum(
        scattered_values * jnp.arange(records_here, dtype=jnp.int32)[:, None], axis=0
    )
    filled = jnp.sum(scattered_values, axis=0).astype(jnp.bfloat16)
    packed_columns = jnp.take(parent_columns, source_row, axis=2)
    packed_cells = jnp.transpose(jnp.take(record_cells, source_row, axis=0))[:, None, :]
    packed_weights = (
        jnp.transpose(jnp.take(record_weights, source_row, axis=0)) * filled[None, :]
    )[:, None, :]
    got_columns, got_cells, got_weights = (
        lax.all_to_all(packed_columns, "gx", split_axis=2, concat_axis=2, tiled=True),
        lax.all_to_all(packed_cells, "gx", split_axis=2, concat_axis=2, tiled=True),
        lax.all_to_all(packed_weights, "gx", split_axis=2, concat_axis=2, tiled=True),
    )
    coarse_ids = jnp.arange(coarse_count, dtype=jnp.int32)
    spread_matrix = jnp.zeros((got_columns.shape[2], coarse_count), jnp.float32)
    for entry in range(got_cells.shape[0]):
        hits = (got_cells[entry, 0][:, None] == coarse_ids[None, :]).astype(jnp.float32)
        spread_matrix = spread_matrix + hits * got_weights[entry, 0].astype(jnp.float32)[:, None]
    coarse = jnp.einsum(
        "vps,sg->vpg",
        got_columns.astype(jnp.float32),
        spread_matrix,
        precision=lax.Precision.HIGHEST,
    )
    heights = terrain[::RATIO, ::RATIO].reshape(-1).astype(jnp.float32)
    vertical = level_weights(heights, levels, parent_columns.shape[1])
    target = jnp.einsum("kpg,vpg->vkg", vertical, coarse, precision=lax.Precision.HIGHEST)
    target = target.reshape(variables, levels, coarse_x, coarse_y)
    target_part = project(target, basis_x[:, ::RATIO], basis_y[:, ::RATIO]) * (
        RATIO * RATIO * scale
    )
    nest_part = project(fields, basis_x, basis_y) * scale
    nest_total, target_total = lax.psum((nest_part, target_part), ("gx", "gy"))
    nudge_coeffs = nest_total - target_total
    low_modes = expand(nudge_coeffs, basis_x, basis_y) * scale
    padded = padded_2(fields, (("gx", 2), ("gy", 3)), 1)
    inv_metric = jnp.square(top_height / (top_height - terrain.astype(jnp.float32)))
    updated_state = advance(padded, fields, fields[0:1], fields[1:2], inv_metric, low_modes)
    return (updated_state, nudge_coeffs)


def solution(mesh):
    return jax.shard_map(
        per_device,
        mesh=mesh,
        in_specs=(
            P(None, None, "gx", "gy"),
            P("gx", "gy"),
            P(None, None, ("gx", "gy")),
            P(("gx", "gy"), None),
            P(("gx", "gy"), None),
            P(("gx", "gy"), None),
        ),
        out_specs=(P(None, None, "gx", "gy"), P()),
        check_vma=False,
    )
```

profile of v0, /device:TPU:1, one launch (start us, length us, event | category | flops | bytes accessed | tf_op | source)
XLA Modules:
  0.0 654.5 jit_solution(16621473508492670728)
XLA Ops:
  7.2 1.6 fusion.66
  8.7 5.6 collective-permute-start.1
  14.3 8.7 %collective-permute-start = (f32[3,8,1,128]{3,2,1,0:T(1,128)}, f32[3,8,1,128]{3,2,1,0:T(1,128)}, u32[]{:S(2)}, u32[]{:S(2)}) collective-permute-start(f32[3,8,1,128]{3,2,1,0:T(1,128)} %get-tuple-element.23), channel_id=1, source_target_pairs={{24,0},{48,24},{72,48},{96,72},{120,96},{144,120},{168,144},{192,1... | collective-permute-start | bytes 36872 | tf_op jit(solution)/shard_map/ppermute | solution.py:25
  26.9 1.9 gather_fusion.2
  30.1 4.6 all-to-all-start.2
  37.0 1.6 fusion.68
  41.6 1.6 gather_fusion.1
  45.3 2.8 gather_fusion
  48.2 3.2 fusion.69
  53.9 1.6 reshape.304
  55.5 10.4 %all-to-all-start.1 = ((s32[4,1,768]{0,1,2:T(1,128)}), s32[4,1,768]{0,1,2:T(1,128)S(1)}, u32[]{:S(2)}, u32[]{:S(2)}) async-start(s32[4,1,768]{0,1,2:T(1,128)} %bitcast.11), calls=%async_computation.1 | async-start | bytes 786432 | tf_op jit(solution)/shard_map/all_to_all | solution.py:145
  65.9 11.9 %fusion.22 = (f32[768]{0:T(1024)S(1)}, f32[768]{0:T(1024)S(1)}, f32[768]{0:T(1024)S(1)}, f32[768]{0:T(1024)S(1)}) fusion(bf16[4,1,768]{0,1,2:T(2,128)(2,1)S(1)} %all-to-all-done.2), kind=kLoop, calls=%fused_computation.56 | loop fusion | flops 3072 | bytes 18432 | tf_op jit(solution)/shard_map/convert_element_type | solution.py:152
  78.7 2.8 all-to-all-done.1
  81.4 7.0 %all-to-all-start = ((bf16[32,2,2160]{2,1,0:T(2,128)(2,1)}), bf16[32,2,2160]{2,1,0:T(2,128)(2,1)S(1)}, u32[]{:S(2)}, u32[]{:S(2)}) async-start(bf16[32,2,2160]{2,1,0:T(2,128)(2,1)} %reshape.304), calls=%async_computation | async-start | bytes 557056 | tf_op jit(solution)/shard_map/all_to_all | solution.py:144
  88.5 1.9 fusion.65
  90.4 1.8 copy.89
  94.0 4.2 collective-permute-start.3
  98.2 57.9 %slice_reduce_fusion.3 = (s32[768]{0:T(1024)S(1)}, s32[768]{0:T(1024)S(1)}, s32[768]{0:T(1024)S(1)}, s32[768]{0:T(1024)S(1)}) fusion(s32[4,1,768]{0,1,2:T(1,128)S(1)} %all-to-all-done.1), kind=kLoop, calls=%fused_computation.57 | loop fusion | bytes 24576 | tf_op jit(solution)/shard_map/slice | solution.py:151
  158.5 2.1 fusion.6
  161.2 1.6 convolution_multiply_fusion.1
  164.0 2.3 copy.88
  166.4 474.7 %all-reduce.3.cloned.1.call-done = (f32[3,8,32,32]{3,2,1,0:T(8,128)}, f32[3,8,32,32]{3,2,1,0:T(8,128)}) async-done(((f32[3,8,32,32]{3,2,1,0:T(8,128)}, f32[3,8,32,32]{3,2,1,0:T(8,128)}), (f32[3,8,32,32]{3,2,1,0:T(8,128)}, f32[3,8,32,32]{3,2,1,0:T(8,128)})) %all-reduce.3.cloned.1.call-update) | async-done | bytes 196624 | tf_op jit(solution)/shard_map/psum | solution.py:167
  641.1 1.3 sub.106
  642.9 4.5 fusion.1
  (124 shorter events, 22.0 us)
Async XLA Ops:
  8.7 69.1 %collective-permute-start.1 = (f32[3,8,1,128]{3,2,1,0:T(1,128)}, f32[3,8,1,128]{3,2,1,0:T(1,128)}, u32[]{:S(2)}, u32[]{:S(2)}) collective-permute-start(f32[3,8,1,128]{3,2,1,0:T(1,128)} %get-tuple-element.22), channel_id=1, source_target_pairs={{0,24},{24,48},{48,72},{72,96},{96,120},{120,144},{144,168},{168,1... | collective-permute-start | bytes 36872 | tf_op jit(solution)/shard_map/ppermute | solution.py:23
  14.3 63.5 %collective-permute-start = (f32[3,8,1,128]{3,2,1,0:T(1,128)}, f32[3,8,1,128]{3,2,1,0:T(1,128)}, u32[]{:S(2)}, u32[]{:S(2)}) collective-permute-start(f32[3,8,1,128]{3,2,1,0:T(1,128)} %get-tuple-element.23), channel_id=1, source_target_pairs={{24,0},{48,24},{72,48},{96,72},{120,96},{144,120},{168,144},{192,1... | collective-permute-start | bytes 36872 | tf_op jit(solution)/shard_map/ppermute | solution.py:25
  26.0 17.2 %copy-start.14 = (pred[768]{0:T(1024)(128)(4,1)}, pred[768]{0:T(1024)(128)(4,1)S(1)}, u32[]{:S(2)}) copy-start(pred[768]{0:T(1024)(128)(4,1)S(1)} %compare_and_fusion) | copy-start | bytes 2308
  28.8 6.5 copy-start
  30.1 25.4 %all-to-all-start.2 = ((bf16[4,1,768]{0,1,2:T(2,128)(2,1)}), bf16[4,1,768]{0,1,2:T(2,128)(2,1)S(1)}, u32[]{:S(2)}, u32[]{:S(2)}) async-start(bf16[4,1,768]{0,1,2:T(2,128)(2,1)} %copy.96), calls=%async_computation.2 | async-start | bytes 786432 | tf_op jit(solution)/shard_map/all_to_all | solution.py:146
  34.7 9.4 %copy-start.18 = (s32[32]{0:T(128)}, s32[32]{0:T(128)S(1)}, u32[]{:S(2)}) copy-start(s32[32]{0:T(128)S(1)} %add_select_fusion.4) | copy-start | bytes 388
  35.3 8.8 %copy-start.23 = (pred[32]{0:T(512)(128)(4,1)}, pred[32]{0:T(512)(128)(4,1)S(1)}, u32[]{:S(2)}) copy-start(pred[32]{0:T(512)(128)(4,1)S(1)} %get-tuple-element.28) | copy-start | bytes 100
  35.3 8.8 %copy-start.25 = (pred[32]{0:T(512)(128)(4,1)}, pred[32]{0:T(512)(128)(4,1)S(1)}, u32[]{:S(2)}) copy-start(pred[32]{0:T(512)(128)(4,1)S(1)} %get-tuple-element.29) | copy-start | bytes 100
  37.0 4.5 copy-start.20
  48.1 3.3 copy-start.12
  48.2 3.3 copy-start.13
  48.2 3.3 copy-start.19
  48.2 3.3 copy-start.24
  48.2 3.3 copy-start.26
  48.2 4.7 copy-start.5
  48.2 4.7 copy-start.16
  48.2 4.7 copy-start.29
  55.5 25.9 %all-to-all-start.1 = ((s32[4,1,768]{0,1,2:T(1,128)}), s32[4,1,768]{0,1,2:T(1,128)S(1)}, u32[]{:S(2)}, u32[]{:S(2)}) async-start(s32[4,1,768]{0,1,2:T(1,128)} %bitcast.11), calls=%async_computation.1 | async-start | bytes 786432 | tf_op jit(solution)/shard_map/all_to_all | solution.py:145
  81.4 74.7 %all-to-all-start = ((bf16[32,2,2160]{2,1,0:T(2,128)(2,1)}), bf16[32,2,2160]{2,1,0:T(2,128)(2,1)S(1)}, u32[]{:S(2)}, u32[]{:S(2)}) async-start(bf16[32,2,2160]{2,1,0:T(2,128)(2,1)} %reshape.304), calls=%async_computation | async-start | bytes 557056 | tf_op jit(solution)/shard_map/all_to_all | solution.py:144
  88.5 552.6 %all-reduce.3.cloned.1.call-start = ((), (), s32[]{:S(2)}) async-start(), calls=%async_computation.3 | async-start | bytes 1572864 | tf_op jit(solution)/shard_map/psum | solution.py:167
  92.7 71.3 %collective-permute-start.2 = (f32[3,8,98,1]{2,1,3,0:T(8,128)S(1)}, f32[3,8,98,1]{2,1,3,0:T(8,128)}, u32[]{:S(2)}, u32[]{:S(2)}) collective-permute-start(f32[3,8,98,1]{2,1,3,0:T(8,128)S(1)} %copy.87), channel_id=1, source_target_pairs={{1,0},{2,1},{3,2},{4,3},{5,4},{6,5},{7,6},{8,7},{9,8},{10,9},{11,1... | collective-permute-start | bytes 28232 | tf_op jit(solution)/shard_map/ppermute | solution.py:25
  94.0 69.5 %collective-permute-start.3 = (f32[3,8,98,1]{2,1,3,0:T(8,128)S(1)}, f32[3,8,98,1]{2,1,3,0:T(8,128)S(1)}, u32[]{:S(2)}, u32[]{:S(2)}) collective-permute-start(f32[3,8,98,1]{2,1,3,0:T(8,128)S(1)} %copy.89), channel_id=1, source_target_pairs={{0,1},{1,2},{2,3},{3,4},{4,5},{5,6},{6,7},{7,8},{8,9},{9,10},{10,1... | collective-permute-start | bytes 28232 | tf_op jit(solution)/shard_map/ppermute | solution.py:23
  164.0 478.9 %copy-start.4 = (f32[3,7,96,128]{3,2,1,0:T(8,128)S(1)}, f32[3,7,96,128]{3,2,1,0:T(8,128)}, u32[]{:S(2)}) copy-start(f32[3,7,96,128]{3,2,1,0:T(8,128)} %get-tuple-element.26) | copy-start | bytes 3096580
  642.4 5.0 copy-start.2
  (15 other events, 28.6 us)
Sparse Core Ops, SparseCore 0:
  163.0 478.0 all-reduce.2
where the time goes:
time: 662 us; the launch traced here: 655 us
  waiting for transfers between devices  478 us (72%)
  local copies, waits for them, and re-layouts  84 us (13%)
  starting transfers between devices  41.8 us (6%)
  other arithmetic  24.5 us (4%)
  between operations  14.9 us (2%)
  matrix products  11.8 us (2%)
    psum x1, waiting for transfers between devices, per_device(): nest_total, target_total = lax.psum((nest_part, target_part), ('gx', 'gy'))  475 us
    slice x1, local copies, waits for them, and re-layouts, per_device(): got_cells[entry, 0][:, None] == coarse_ids[None, :]  57.9 us
  transfers between devices with their start and end apart: 8, of which 2 were waited for; matrix products, arithmetic and copies ran while one was open for 17% of the time, Pallas kernels for 0%

commit v1 on v0

v1 whole, which is shorter than its diff:
```python
import functools

import jax
import jax.numpy as jnp
import numpy as np
from jax import lax
from jax.experimental import pallas as pl
from jax.experimental.pallas import tpu as pltpu
from jax.sharding import PartitionSpec as P

KW = 32
RATIO = 8
TOP = 12000.0
LANES = 128
EXACT = lax.Precision.HIGHEST


def wave_rows(length):
    half = KW // 2
    x = np.arange(length)
    rows = [np.ones(length)]
    for m in range(1, half):
        rows.append(np.sqrt(2.0) * np.cos(2.0 * np.pi * (m * x % length) / length))
    for m in range(half, KW):
        rows.append(np.sqrt(2.0) * np.sin(2.0 * np.pi * ((m - half + 1) * x % length) / length))
    return np.stack(rows)


def two_parts(table):
    whole = table.astype(np.float32)
    high = whole.astype(jnp.bfloat16)
    low = (whole - high.astype(np.float32)).astype(jnp.bfloat16)
    return np.concatenate([high, low], axis=-2)


def dot(a, b, dims=((1,), (0,)), precision=None):
    return lax.dot_general(
        a, b, (dims, ((), ())), precision=precision, preferred_element_type=jnp.float32
    )


def rows_lanes(shape):
    return (
        lax.broadcasted_iota(jnp.int32, shape, 0),
        lax.broadcasted_iota(jnp.int32, shape, 1),
    )


def nest_kernel(here, f_ref, bx_ref, by_ref, p_ref, x0_ref, x1_ref, y0_ref, y1_ref):
    count, cells_x, cells_y = f_ref.shape
    per = LANES // KW
    row, lane = rows_lanes((cells_y, LANES))
    by4 = by_ref[0]
    spread = jnp.concatenate(
        [jnp.where(lane // KW == q, by4, 0.0) for q in range(per)], axis=0
    )
    bx = bx_ref[0]
    for g in range(count // per):
        values = jnp.concatenate([f_ref[per * g + q] for q in range(per)], axis=1)
        along_y = dot(values, spread, precision=EXACT)
        p_ref[:, pl.ds(g * LANES, LANES)] = dot(bx, along_y, precision=EXACT)
    row, lane = rows_lanes((cells_x, cells_y))
    for i in range(count):
        q = f_ref[i]
        x0_ref[i : i + 1, :] = q[0:1, :]
        x1_ref[i : i + 1, :] = q[cells_x - 1 : cells_x, :]
        for ref, at in ((y0_ref, 0), (y1_ref, cells_y - 1)):
            edge = jnp.broadcast_to(q[:, at : at + 1], q.shape)
            ref[i : i + 1, :] = jnp.sum(jnp.where(row == lane, edge, 0.0), axis=0, keepdims=True)


def record_kernel(
    here, h_ref, tile_ref, cells_ref, weights_ref, cols_ref, tabx_ref, taby_ref, p_ref, d_ref,
    col_ref, pick_ref, acc_ref, acc2_ref, *, levels, coarse_x, coarse_y, scale
):
    variables, parents, records = cols_ref.shape
    tiles = h_ref.shape[0]
    padded = h_ref.shape[1]
    coarse_all = tabx_ref.shape[1]
    for v in range(variables):
        col_ref[v] = cols_ref[v].astype(jnp.float32)
    tile = tile_ref[...]
    row, _ = rows_lanes((tiles, records))
    tile_hot = (row == tile).astype(jnp.float32).astype(jnp.bfloat16)
    heights = h_ref[...]
    high = jnp.floor(heights * (1.0 / 64.0))
    low = heights - 64.0 * high
    over = ((0,), (0,))
    pick_ref[...] = 64.0 * dot(high.astype(jnp.bfloat16), tile_hot, over) + dot(
        low.astype(jnp.bfloat16), tile_hot, over
    )
    acc_ref[...] = jnp.zeros_like(acc_ref)
    acc2_ref[...] = jnp.zeros_like(acc2_ref)
    row_c, _ = rows_lanes((padded, records))
    row_a, _ = rows_lanes((coarse_all, records))
    row_b, _ = rows_lanes((coarse_y, records))
    row_p, _ = rows_lanes((parents, records))
    parent = (row_p.astype(jnp.float32) + 0.5) * (TOP / parents)

    def entry(e, carry):
        cell = cells_ref[pl.ds(e, 1), :]
        weight = weights_ref[pl.ds(e, 1), :]
        height = jnp.sum(jnp.where(row_c == cell, pick_ref[...], 0.0), axis=0, keepdims=True)
        inner_x = cell // coarse_y
        a_hot = (row_a == tile * coarse_x + inner_x).astype(jnp.float32).astype(jnp.bfloat16)
        b_hot = (row_b == cell - inner_x * coarse_y).astype(jnp.float32).astype(jnp.bfloat16)
        bx2 = dot(tabx_ref[...], a_hot).astype(jnp.bfloat16)
        by2 = dot(taby_ref[0], b_hot)
        by = by2[:KW] + by2[KW:]
        spacing = (TOP - height) * (1.0 / levels)
        inverse = 1.0 / spacing
        apart = parent * inverse - (height * inverse + 0.5)
        uppers, lowers = [], []
        parts = [[None] * levels for _ in range(variables)]
        for k in range(levels):
            hat = jnp.maximum(0.0, 1.0 - jnp.abs(apart - float(k)))
            share = weight / jnp.sum(hat, axis=0, keepdims=True)
            for v in range(variables):
                parts[v][k] = jnp.sum(hat * col_ref[v], axis=0, keepdims=True) * share
        for v in range(variables):
            for k in range(levels):
                both = by * parts[v][k]
                upper = both.astype(jnp.bfloat16)
                uppers.append(upper)
                lowers.append((both - upper.astype(jnp.float32)).astype(jnp.bfloat16))
        last = ((1,), (1,))
        acc_ref[...] += dot(bx2, jnp.concatenate(uppers, axis=0), last)
        acc2_ref[...] += dot(bx2[:KW], jnp.concatenate(lowers, axis=0), last)
        return carry

    lax.fori_loop(0, cells_ref.shape[0], entry, 0)
    target = acc_ref[:KW] + acc_ref[KW:] + acc2_ref[...]
    d_ref[...] = p_ref[...] * scale - target * (RATIO * RATIO * scale)


def advance_kernel(
    here, f_ref, terrain_ref, n_ref, west_ref, east_ref, south_ref, north_ref, bx_ref, by_ref,
    out_ref, coeffs_ref, *, variables
):
    count, cells_x, cells_y = f_ref.shape
    levels = count // variables
    per = LANES // KW
    row, lane = rows_lanes((cells_x, cells_y))
    by4 = by_ref[0]
    block, _ = rows_lanes(by4.shape)
    nudge = n_ref[...]
    for i in range(count):
        coeffs_ref[i] = nudge[:, i * KW : (i + 1) * KW]
    along_x = dot(bx_ref[0], nudge, precision=EXACT)
    south = jnp.transpose(south_ref[...])
    north = jnp.transpose(north_ref[...])
    metric = TOP / (TOP - terrain_ref[...].astype(jnp.float32))
    metric = metric * metric * 0.1
    spreads = [jnp.where(block // KW == q, by4, 0.0) for q in range(per)]
    for i in range(count):
        k = i % levels
        q = f_ref[i]
        wind_x = f_ref[k]
        wind_y = f_ref[levels + k]
        east = jnp.where(row == cells_x - 1, east_ref[i : i + 1, :], pltpu.roll(q, cells_x - 1, 0))
        west = jnp.where(row == 0, west_ref[i : i + 1, :], pltpu.roll(q, 1, 0))
        above = jnp.where(lane == cells_y - 1, north[:cells_x, i : i + 1], pltpu.roll(q, cells_y - 1, 1))
        below = jnp.where(lane == 0, south[:cells_x, i : i + 1], pltpu.roll(q, 1, 1))
        transport = wind_x * (east - west) + wind_y * (above - below)
        diffusion = east + west + above + below - 4.0 * q
        upper = f_ref[i + 1] if k < levels - 1 else q
        lower = f_ref[i - 1] if k > 0 else q
        mixing = (upper - 2.0 * q + lower) * metric
        g = i // per
        low = dot(along_x[:, g * LANES : (g + 1) * LANES], spreads[i % per], precision=EXACT)
        out_ref[i] = q - 0.05 * transport + 0.1 * diffusion + mixing + low


def whole(shape):
    return pl.BlockSpec(shape, lambda i, here: (0,) * len(shape))


def picked(shape, which):
    return pl.BlockSpec((1,) + shape, lambda i, here: (here[which],) + (0,) * len(shape))


def call(kernel, here, ins, specs, outs, scratch=()):
    return pl.pallas_call(
        kernel,
        out_shape=[jax.ShapeDtypeStruct(s, jnp.float32) for s in outs],
        grid_spec=pltpu.PrefetchScalarGridSpec(
            num_scalar_prefetch=1,
            grid=(1,),
            in_specs=specs,
            out_specs=[whole(s) for s in outs],
            scratch_shapes=list(scratch),
        ),
        compiler_params=pltpu.CompilerParams(vmem_limit_bytes=48 << 20),
    )(here, *ins)


def gather(piece, axis):
    count = lax.axis_size(axis)
    return lax.all_to_all(
        jnp.broadcast_to(piece[None], (count,) + piece.shape), axis, 0, 0, tiled=True
    )


def shift(piece, axis, step):
    count = lax.axis_size(axis)
    return lax.ppermute(
        piece, axis, [(i, i + step) for i in range(count) if 0 <= i + step < count]
    )


def summed(part):
    count = lax.axis_size("gx")
    pieces = part.reshape(count, part.size // (count * LANES), LANES)
    mine = jnp.sum(lax.all_to_all(pieces, "gx", 0, 0, tiled=True), axis=0)
    mine = jnp.sum(gather(mine, "gy"), axis=0)
    return gather(mine, "gx").reshape(part.shape)


def per_device(fields, terrain, columns, record_tile, record_cells, record_weights):
    tiles_x, tiles_y = lax.axis_size("gx"), lax.axis_size("gy")
    variables, levels, cells_x, cells_y = fields.shape
    total_x, total_y = cells_x * tiles_x, cells_y * tiles_y
    coarse_x, coarse_y = cells_x // RATIO, cells_y // RATIO
    count = variables * levels
    wide = count * KW
    parents, records = columns.shape[1:]
    scale = 1.0 / np.sqrt(total_x * total_y)
    wave_x, wave_y = wave_rows(total_x), wave_rows(total_y)
    per = LANES // KW
    by_x = wave_x.reshape(KW, tiles_x, cells_x).transpose(1, 0, 2)
    by_y = wave_y.reshape(KW, tiles_y, cells_y).transpose(1, 0, 2)
    tab_bx = by_x.astype(np.float32)
    tab_bxt = (-4.0 * scale * by_x.transpose(0, 2, 1)).astype(np.float32)
    tab_by = np.tile(by_y, (1, per, 1)).astype(np.float32)
    tab_byt = np.tile(by_y.transpose(0, 2, 1), (1, 1, per)).astype(np.float32)
    tab_ax = two_parts(wave_x[:, ::RATIO])
    tab_ay = two_parts(by_y[:, :, ::RATIO])

    here = jnp.stack([lax.axis_index("gx"), lax.axis_index("gy")]).astype(jnp.int32)
    f = fields.reshape(count, cells_x, cells_y)

    coarse = coarse_x * coarse_y
    padded = -(-coarse // LANES) * LANES
    own = terrain[::RATIO, ::RATIO].astype(jnp.float32).reshape(coarse)
    own = jnp.pad(own, (0, padded - coarse)).reshape(padded // LANES, LANES)
    heights = gather(own, "gx").reshape(tiles_x, padded)

    nest, x0, x1, y0, y1 = call(
        nest_kernel,
        here,
        (f, tab_bx, tab_byt),
        [whole(f.shape), picked((KW, cells_x), 0), picked((cells_y, LANES), 1)],
        [(KW, wide)] + [(count, cells_y)] * 4,
    )
    west, east = shift(x1, "gx", 1), shift(x0, "gx", -1)
    south, north = shift(y1, "gy", 1), shift(y0, "gy", -1)

    flat = [record_tile.T, record_cells.T, record_weights.T.astype(jnp.float32)]
    (part,) = call(
        functools.partial(
            record_kernel, levels=levels, coarse_x=coarse_x, coarse_y=coarse_y, scale=scale
        ),
        here,
        (heights, *flat, columns, tab_ax, tab_ay, nest),
        [whole(heights.shape)]
        + [whole(x.shape) for x in flat]
        + [whole(columns.shape), whole(tab_ax.shape), picked(tab_ay.shape[1:], 1), whole(nest.shape)],
        [(KW, wide)],
        [
            pltpu.VMEM((variables, parents, records), jnp.float32),
            pltpu.VMEM((padded, records), jnp.float32),
            pltpu.VMEM((2 * KW, wide), jnp.float32),
            pltpu.VMEM((KW, wide), jnp.float32),
        ],
    )
    nudge = summed(part)

    updated, coeffs = call(
        functools.partial(advance_kernel, variables=variables),
        here,
        (f, terrain, nudge, west, east, south, north, tab_bxt, tab_by),
        [whole(x.shape) for x in (f, terrain, nudge, west, east, south, north)]
        + [picked((cells_x, KW), 0), picked((LANES, cells_y), 1)],
        [f.shape, (count, KW, KW)],
    )
    return updated.reshape(fields.shape), coeffs.reshape(variables, levels, KW, KW)


def solution(mesh):
    return jax.shard_map(
        per_device,
        mesh=mesh,
        in_specs=(
            P(None, None, "gx", "gy"),
            P("gx", "gy"),
            P(None, None, ("gx", "gy")),
            P(("gx", "gy"), None),
            P(("gx", "gy"), None),
            P(("gx", "gy"), None),
        ),
        out_specs=(P(None, None, "gx", "gy"), P()),
        check_vma=False,
    )
```

time: 662 us -> 105 us (0.16)
  the two profiles are of different devices: /device:TPU:1 before, /device:TPU:6 now
where the time goes in v1:
time: 105 us; the launch traced here: 104 us
  blocking collectives  42.8 us (41%)
  starting transfers between devices  31.9 us (30%)
  local copies, waits for them, and re-layouts  12.6 us (12%)
  Pallas kernels  10.7 us (10%)
  waiting for transfers between devices  4.45 us (4%)
    all_to_all x1, blocking collectives, gather(): lax.all_to_all(jnp.broadcast_to(piece[None], (count,) + piece.shape), axi...  24.6 us
    all_to_all x2, starting transfers between devices, gather(): lax.all_to_all(jnp.broadcast_to(piece[None], (count,) + piece.shape), axi...  19.3 us
    all_to_all x1, blocking collectives, summed(): mine = jnp.sum(lax.all_to_all(pieces, 'gx', 0, 0, tiled=True), axis=0)  18.1 us
    ppermute x4, starting transfers between devices, shift(): lax.ppermute(piece, axis, [(i, i + step) for i in range(count) if 0 <= i...  12.6 us
    pallas_call x3, Pallas kernels, call(): pl.pallas_call(kernel, out_shape=[jax.ShapeDtypeStruct(s, jnp.float32) fo...  10.7 us
    unnamed x40, local copies, waits for them, and re-layouts  10.3 us
    ppermute x4, waiting for transfers between devices, shift(): lax.ppermute(piece, axis, [(i, i + step) for i in range(count) if 0 <= i...  4.44 us
  transfers between devices with their start and end apart: 6, of which 2 were waited for; matrix products, arithmetic and copies ran while one was open for 1% of the time, Pallas kernels for 3%

profile of v1, /device:TPU:6, one launch (start us, length us, event | category | flops | bytes accessed | tf_op | source)
XLA Modules:
  0.0 104.1 jit_solution(6977149583919755540)
XLA Ops:
  0.6 0.9 slice.3
  1.6 0.6 broadcast_in_dim.9
  2.3 13.2 %all-to-all-start = ((f32[32,2,128]{2,1,0:T(2,128)}), f32[32,2,128]{2,1,0:T(2,128)S(1)}, u32[]{:S(2)}, u32[]{:S(2)}) async-start(f32[32,2,128]{2,1,0:T(2,128)} %broadcast_in_dim.9), calls=%async_computation | async-start | bytes 65536 | tf_op jit(solution)/shard_map/all_to_all | solution.py:199
  15.4 0.7 convert_bitcast_fusion.weights_ref
  16.7 1.3 %copy-done = f32[3,8,96,128]{3,2,1,0:T(8,128)S(1)} copy-done((f32[3,8,96,128]{3,2,1,0:T(8,128)S(1)}, f32[3,8,96,128]{3,2,1,0:T(8,128)}, u32[]{:S(2)}) %copy-start) | copy-done | bytes 1179672
  18.0 1.4 %copy-done.4 = f32[24,128,128]{2,1,0:T(8,128)S(1)} copy-done((f32[24,128,128]{2,1,0:T(8,128)S(1)}, f32[24,128,128]{2,1,0:T(8,128)}, u32[]{:S(2)}) %copy-start.4) | copy-done | bytes 1572888
  19.4 1.0 copy-done.5
  20.4 2.7 %shard_map.131 = (f32[32,768]{1,0:T(8,128)S(1)}, f32[24,128]{1,0:T(8,128)S(1)}, f32[24,128]{1,0:T(8,128)S(1)}, f32[24,128]{1,0:T(8,128)S(1)}, f32[24,128]{1,0:T(8,128)S(1)}) custom-call(s32[2]{0:T(128)S(1)} %pad_add_fusion.here, f32[24,96,128]{2,1,0:T(8,128)S(1)} %bitcast.19, f32[32,32,96]{2,1,0:T(8,128)S(1)} %copy-done.5, f32[24,128,128]{2,1,0:T(8,128)S(1)} %copy-done.4), custom_call_target="tpu_custom_call" | custom-call | tf_op jit(solution)/shard_map/pallas_call | solution.py:183
  23.2 0.6 copy-done.15
  25.6 0.9 copy-done.9
  26.5 0.6 copy-done.12
  27.1 0.7 copy-done.14
  27.8 4.5 %shard_map.132 = f32[32,768]{1,0:T(8,128)S(1)} custom-call(s32[2]{0:T(128)S(1)} %copy-done.12, f32[32,256]{1,0:T(8,128)S(1)} %bitcast.22, s32[1,384]{1,0:T(1,128)S(1)} %bitcast.24, s32[4,384]{1,0:T(4,128)S(1)} %bitcast.23, f32[4,384]{1,0:T(4,128)S(1)} %convert_bitcast_fusion.weights_ref, bf16[3,60,384]{2,1,0:T(8,128)(2,1)S(1)} %copy-done.7, ...), custom_call_target="tpu_custom_call" | custom-call | tf_op jit(solution)/shard_map/pallas_call | solution.py:183
  32.4 18.1 %all_to_all.20 = f32[32,6,128]{2,1,0:T(8,128)S(1)} all-to-all(f32[32,6,128]{2,1,0:T(8,128)S(1)} %reshape.31), channel_id=1, replica_groups=mesh['gx'=32,'gy'=24] {'gx'}, dimensions={0} | all-to-all | bytes 196608 | tf_op jit(solution)/shard_map/all_to_all | solution.py:214
  50.5 24.6 %all_to_all.21 = f32[24,6,128]{2,1,0:T(8,128)S(1)} all-to-all(f32[24,6,128]{2,1,0:T(8,128)S(1)} %broadcast_in_dim.10), channel_id=1, replica_groups=mesh['gx'=32,'gy'=24] {'gy'}, dimensions={0} | all-to-all | bytes 147456 | tf_op jit(solution)/shard_map/all_to_all | solution.py:199
  75.2 0.7 broadcast_in_dim.22
  75.9 6.1 %all-to-all-start.3 = ((f32[32,6,128]{2,1,0:T(8,128)}), f32[32,6,128]{2,1,0:T(8,128)S(1)}, u32[]{:S(2)}, u32[]{:S(2)}) async-start(f32[32,6,128]{2,1,0:T(8,128)} %broadcast_in_dim.22), calls=%async_computation.3 | async-start | bytes 262144 | tf_op jit(solution)/shard_map/all_to_all | solution.py:199
  82.0 2.1 %collective-permute-start = (f32[24,128]{1,0:T(8,128)}, f32[24,128]{1,0:T(8,128)S(1)}, u32[]{:S(2)}, u32[]{:S(2)}) collective-permute-start(f32[24,128]{1,0:T(8,128)} %copy-done.18), channel_id=1, source_target_pairs={{0,24},{24,48},{48,72},{72,96},{96,120},{120,144},{144,168},{168,1... | collective-permute-start | bytes 36872 | tf_op jit(solution)/shard_map/ppermute | solution.py:206
  84.1 6.5 %collective-permute-start.1 = (f32[24,128]{1,0:T(8,128)}, f32[24,128]{1,0:T(8,128)S(1)}, u32[]{:S(2)}, u32[]{:S(2)}) collective-permute-start(f32[24,128]{1,0:T(8,128)} %copy-done.17), channel_id=1, source_target_pairs={{24,0},{48,24},{72,48},{96,72},{120,96},{144,120},{168,144},{192,1... | collective-permute-start | bytes 36872 | tf_op jit(solution)/shard_map/ppermute | solution.py:206
  90.6 2.8 %collective-permute-start.2 = (f32[24,128]{1,0:T(8,128)}, f32[24,128]{1,0:T(8,128)S(1)}, u32[]{:S(2)}, u32[]{:S(2)}) collective-permute-start(f32[24,128]{1,0:T(8,128)} %copy-done.16), channel_id=1, source_target_pairs={{0,1},{1,2},{2,3},{3,4},{4,5},{5,6},{6,7},{7,8},{8,9},{9,10},{10,1... | collective-permute-start | bytes 36872 | tf_op jit(solution)/shard_map/ppermute | solution.py:206
  93.4 1.3 %collective-permute-start.3 = (f32[24,128]{1,0:T(8,128)}, f32[24,128]{1,0:T(8,128)S(1)}, u32[]{:S(2)}, u32[]{:S(2)}) collective-permute-start(f32[24,128]{1,0:T(8,128)} %copy-done.15), channel_id=1, source_target_pairs={{1,0},{2,1},{3,2},{4,3},{5,4},{6,5},{7,6},{8,7},{9,8},{10,9},{11,1... | collective-permute-start | bytes 36872 | tf_op jit(solution)/shard_map/ppermute | solution.py:206
  95.0 4.2 %collective-permute-done.3.north_ref = f32[24,128]{1,0:T(8,128)S(1)} collective-permute-done((f32[24,128]{1,0:T(8,128)}, f32[24,128]{1,0:T(8,128)S(1)}, u32[]{:S(2)}, u32[]{:S(2)}) %collective-permute-start.3) | collective-permute-done | bytes 12320 | tf_op jit(solution)/shard_map/ppermute | solution.py:206
  99.2 1.4 %copy-done.3 = f32[32,96,32]{2,1,0:T(8,128)S(1)} copy-done((f32[32,96,32]{2,1,0:T(8,128)S(1)}, f32[32,96,32]{2,1,0:T(8,128)}, u32[]{:S(2)}) %copy-start.3) | copy-done | bytes 393240
  100.6 3.4 %shard_map.133 = (f32[24,96,128]{2,1,0:T(8,128)}, f32[24,32,32]{2,1,0:T(8,128)}) custom-call(s32[2]{0:T(128)S(1)} %copy-done.13, f32[24,96,128]{2,1,0:T(8,128)S(1)} %bitcast.20, s32[96,128]{1,0:T(8,128)S(1)} %copy-done.8, f32[32,768]{1,0:T(8,128)S(1)} %bitcast.21, f32[24,128]{1,0:T(8,128)S(1)} %collective-permute-done.west_ref, ...), custom_call_target="tpu_custom_call" | custom-call | tf_op jit(solution)/shard_map/pallas_call | solution.py:183
  (45 shorter events, 2.9 us)
Async XLA Ops:
  2.3 23.3 %all-to-all-start = ((f32[32,2,128]{2,1,0:T(2,128)}), f32[32,2,128]{2,1,0:T(2,128)S(1)}, u32[]{:S(2)}, u32[]{:S(2)}) async-start(f32[32,2,128]{2,1,0:T(2,128)} %broadcast_in_dim.9), calls=%async_computation | async-start | bytes 65536 | tf_op jit(solution)/shard_map/all_to_all | solution.py:199
  16.7 1.3 %copy-start = (f32[3,8,96,128]{3,2,1,0:T(8,128)S(1)}, f32[3,8,96,128]{3,2,1,0:T(8,128)}, u32[]{:S(2)}) copy-start(f32[3,8,96,128]{3,2,1,0:T(8,128)} %param.12) | copy-start | bytes 3538948
  18.0 1.4 %copy-start.4 = (f32[24,128,128]{2,1,0:T(8,128)S(1)}, f32[24,128,128]{2,1,0:T(8,128)}, u32[]{:S(2)}) copy-start(f32[24,128,128]{2,1,0:T(8,128)} %constant.23.clone.by_ref) | copy-start | bytes 4718596
  19.4 1.0 %copy-start.5 = (f32[32,32,96]{2,1,0:T(8,128)S(1)}, f32[32,32,96]{2,1,0:T(8,128)}, u32[]{:S(2)}) copy-start(f32[32,32,96]{2,1,0:T(8,128)} %constant.22.clone.bx_ref) | copy-start | bytes 1179652
  20.4 5.1 %copy-start.6 = (bf16[24,64,16]{2,1,0:T(8,128)(2,1)S(1)}, bf16[24,64,16]{2,1,0:T(8,128)(2,1)}, u32[]{:S(2)}) copy-start(bf16[24,64,16]{2,1,0:T(8,128)(2,1)} %constant.25.clone.taby_ref) | copy-start | bytes 147460
  20.4 5.2 %copy-start.7 = (bf16[3,60,384]{2,1,0:T(8,128)(2,1)S(1)}, bf16[3,60,384]{2,1,0:T(8,128)(2,1)}, u32[]{:S(2)}) copy-start(bf16[3,60,384]{2,1,0:T(8,128)(2,1)} %cols_ref.1) | copy-start | bytes 414724
  20.4 5.2 %copy-start.10 = (s32[384,4]{0,1:T(4,128)S(1)}, s32[384,4]{0,1:T(4,128)}, u32[]{:S(2)}) copy-start(s32[384,4]{0,1:T(4,128)} %param.16) | copy-start | bytes 18436
  20.4 78.8 %copy-start.2 = (f32[24,128,128]{2,1,0:T(8,128)S(1)}, f32[24,128,128]{2,1,0:T(8,128)}, u32[]{:S(2)}) copy-start(f32[24,128,128]{2,1,0:T(8,128)} %constant.27.clone.by_ref) | copy-start | bytes 4718596
  23.2 0.6 copy-start.15
  23.8 0.6 copy-start.16
  24.4 0.6 copy-start.17
  25.0 0.6 copy-start.18
  25.6 73.6 %copy-start.1 = (f32[3,8,96,128]{3,2,1,0:T(8,128)S(1)}, f32[3,8,96,128]{3,2,1,0:T(8,128)}, u32[]{:S(2)}) copy-start(f32[3,8,96,128]{3,2,1,0:T(8,128)} %param.12) | copy-start | bytes 3538948
  25.6 73.6 %copy-start.8 = (s32[96,128]{1,0:T(8,128)S(1)}, s32[96,128]{1,0:T(8,128)}, u32[]{:S(2)}) copy-start(s32[96,128]{1,0:T(8,128)} %terrain_ref.1) | copy-start | bytes 147460
  25.6 0.9 copy-start.9
  26.5 0.6 copy-start.12
  27.1 0.7 copy-start.14
  32.3 66.9 %copy-start.13 = (s32[2]{0:T(128)S(1)}, s32[2]{0:T(128)}, u32[]{:S(2)}) copy-start(s32[2]{0:T(128)} %copy-done.11) | copy-start | bytes 28
  75.9 18.8 %all-to-all-start.3 = ((f32[32,6,128]{2,1,0:T(8,128)}), f32[32,6,128]{2,1,0:T(8,128)S(1)}, u32[]{:S(2)}, u32[]{:S(2)}) async-start(f32[32,6,128]{2,1,0:T(8,128)} %broadcast_in_dim.22), calls=%async_computation.3 | async-start | bytes 262144 | tf_op jit(solution)/shard_map/all_to_all | solution.py:199
  82.0 12.7 %collective-permute-start = (f32[24,128]{1,0:T(8,128)}, f32[24,128]{1,0:T(8,128)S(1)}, u32[]{:S(2)}, u32[]{:S(2)}) collective-permute-start(f32[24,128]{1,0:T(8,128)} %copy-done.18), channel_id=1, source_target_pairs={{0,24},{24,48},{48,72},{72,96},{96,120},{120,144},{144,168},{168,1... | collective-permute-start | bytes 36872 | tf_op jit(solution)/shard_map/ppermute | solution.py:206
  84.1 10.6 %collective-permute-start.1 = (f32[24,128]{1,0:T(8,128)}, f32[24,128]{1,0:T(8,128)S(1)}, u32[]{:S(2)}, u32[]{:S(2)}) collective-permute-start(f32[24,128]{1,0:T(8,128)} %copy-done.17), channel_id=1, source_target_pairs={{24,0},{48,24},{72,48},{96,72},{120,96},{144,120},{168,144},{192,1... | collective-permute-start | bytes 36872 | tf_op jit(solution)/shard_map/ppermute | solution.py:206
  90.6 4.4 %collective-permute-start.2 = (f32[24,128]{1,0:T(8,128)}, f32[24,128]{1,0:T(8,128)S(1)}, u32[]{:S(2)}, u32[]{:S(2)}) collective-permute-start(f32[24,128]{1,0:T(8,128)} %copy-done.16), channel_id=1, source_target_pairs={{0,1},{1,2},{2,3},{3,4},{4,5},{5,6},{6,7},{7,8},{8,9},{9,10},{10,1... | collective-permute-start | bytes 36872 | tf_op jit(solution)/shard_map/ppermute | solution.py:206
  93.4 5.8 %collective-permute-start.3 = (f32[24,128]{1,0:T(8,128)}, f32[24,128]{1,0:T(8,128)S(1)}, u32[]{:S(2)}, u32[]{:S(2)}) collective-permute-start(f32[24,128]{1,0:T(8,128)} %copy-done.15), channel_id=1, source_target_pairs={{1,0},{2,1},{3,2},{4,3},{5,4},{6,5},{7,6},{8,7},{9,8},{10,9},{11,1... | collective-permute-start | bytes 36872 | tf_op jit(solution)/shard_map/ppermute | solution.py:206
  99.2 1.4 %copy-start.3 = (f32[32,96,32]{2,1,0:T(8,128)S(1)}, f32[32,96,32]{2,1,0:T(8,128)}, u32[]{:S(2)}) copy-start(f32[32,96,32]{2,1,0:T(8,128)} %constant.26.clone.bx_ref) | copy-start | bytes 1179652
  (1 other events, 0.5 us)

commit v2 on v1

v2 whole, which is shorter than its diff:
```python
import functools

import jax
import jax.numpy as jnp
import numpy as np
from jax import lax
from jax.experimental import pallas as pl
from jax.experimental.pallas import tpu as pltpu
from jax.sharding import PartitionSpec as P

KW = 32
RATIO = 8
TOP = 12000.0
LANES = 128
EXACT = lax.Precision.HIGHEST


def wave_rows(length):
    half = KW // 2
    x = np.arange(length)
    rows = [np.ones(length)]
    for m in range(1, half):
        rows.append(np.sqrt(2.0) * np.cos(2.0 * np.pi * (m * x % length) / length))
    for m in range(half, KW):
        rows.append(np.sqrt(2.0) * np.sin(2.0 * np.pi * ((m - half + 1) * x % length) / length))
    return np.stack(rows)


def two_parts(table, axis):
    whole = table.astype(np.float32)
    high = whole.astype(jnp.bfloat16)
    low = (whole - high.astype(np.float32)).astype(jnp.bfloat16)
    return np.concatenate([high, low], axis=axis)


def dot(a, b, dims=((1,), (0,)), precision=None):
    return lax.dot_general(
        a, b, (dims, ((), ())), precision=precision, preferred_element_type=jnp.float32
    )


def rows_lanes(shape):
    return (
        lax.broadcasted_iota(jnp.int32, shape, 0),
        lax.broadcasted_iota(jnp.int32, shape, 1),
    )


def split(x):
    high = x.astype(jnp.bfloat16)
    return high, (x - high.astype(jnp.float32)).astype(jnp.bfloat16)


def hot(mask):
    return jnp.where(mask, 1.0, 0.0).astype(jnp.bfloat16)


def ready_kernel(
    f_hbm, bx_hbm, by_hbm, tile_hbm, cells_hbm, tabx_hbm, p_ref, look_ref,
    f_ref, bx_ref, by_ref, tile_ref, cells_ref, tabx_ref, f_sem, bx_sem, by_sem, small_sem,
    *, coarse_x, coarse_y
):
    count, cells_x, cells_y = f_ref.shape
    per = LANES // KW
    groups = count // per
    fetch = [
        pltpu.make_async_copy(f_hbm.at[pl.ds(per * g, per)], f_ref.at[pl.ds(per * g, per)], f_sem.at[g])
        for g in range(groups)
    ]
    by_copy = pltpu.make_async_copy(by_hbm.at[lax.axis_index("gy")], by_ref, by_sem)
    bx_copy = pltpu.make_async_copy(bx_hbm.at[lax.axis_index("gx")], bx_ref, bx_sem)
    small = [
        pltpu.make_async_copy(a, b, small_sem.at[i])
        for i, (a, b) in enumerate(
            ((tile_hbm, tile_ref), (cells_hbm, cells_ref), (tabx_hbm, tabx_ref))
        )
    ]
    for copy in (*small, by_copy, *fetch, bx_copy):
        copy.start()
    for copy in small:
        copy.wait()
    records = tile_ref.shape[1]
    row_a, _ = rows_lanes((tabx_ref.shape[1], records))
    for e in range(cells_ref.shape[0]):
        where_x = tile_ref[...] * coarse_x + cells_ref[e : e + 1, :] // coarse_y
        look_ref[e] = dot(tabx_ref[...], hot(row_a == where_x)).astype(jnp.bfloat16)
    by_copy.wait()
    by4 = by_ref[...].astype(jnp.float32)
    _, lane = rows_lanes(by4.shape)
    spread = jnp.concatenate(
        [
            jnp.where(lane % LANES // KW == q, by4, 0.0).astype(jnp.bfloat16)
            for q in range(per)
        ],
        axis=0,
    )
    along = []
    for g in range(groups):
        fetch[g].wait()
        high, low = split(jnp.concatenate([f_ref[per * g + q] for q in range(per)], axis=1))
        both = dot(high, spread)
        along.append(both[:, :LANES] + both[:, LANES:] + dot(low, spread[:, :LANES]))
    high, low = split(jnp.concatenate(along, axis=1))
    bx_copy.wait()
    both = dot(bx_ref[...], high)
    p_ref[...] = both[:KW] + both[KW:] + dot(bx_ref[:KW, :], low)


def record_kernel(
    h_ref, tile_ref, cells_ref, weights_ref, cols_ref, look_ref, p_ref, taby_hbm, d_ref,
    col_ref, pick_ref, acc_ref, acc2_ref, taby_ref, sem, *, levels, coarse_y, scale
):
    variables, parents, records = cols_ref.shape
    tiles, padded = h_ref.shape
    fetch = pltpu.make_async_copy(taby_hbm.at[lax.axis_index("gy")], taby_ref, sem)
    fetch.start()
    tile = tile_ref[...]
    row, _ = rows_lanes((tiles, records))
    tile_hot = hot(row == tile)
    heights = h_ref[...]
    high = jnp.floor(heights * (1.0 / 64.0))
    low = heights - 64.0 * high
    over = ((0,), (0,))
    pick_ref[...] = 64.0 * dot(high.astype(jnp.bfloat16), tile_hot, over) + dot(
        low.astype(jnp.bfloat16), tile_hot, over
    )
    for v in range(variables):
        col_ref[v] = cols_ref[v].astype(jnp.float32)
    acc_ref[...] = jnp.zeros_like(acc_ref)
    acc2_ref[...] = jnp.zeros_like(acc2_ref)
    row_c, _ = rows_lanes((padded, records))
    row_b, _ = rows_lanes((coarse_y, records))
    row_p, _ = rows_lanes((parents, records))
    parent = (row_p.astype(jnp.float32) + 0.5) * (TOP / parents)
    last = ((1,), (1,))

    def entry(e, carry):
        cell = cells_ref[pl.ds(e, 1), :]
        weight = weights_ref[pl.ds(e, 1), :]
        height = jnp.sum(jnp.where(row_c == cell, pick_ref[...], 0.0), axis=0, keepdims=True)
        in_b = row_b == cell % coarse_y
        inverse = levels / (TOP - height)
        apart = parent * inverse - (height * inverse + 0.5)
        highs = [[None] * levels for _ in range(variables)]
        lows = [[None] * levels for _ in range(variables)]
        for k in range(levels):
            hat = jnp.maximum(0.0, 1.0 - jnp.abs(apart - float(k)))
            share = weight / jnp.sum(hat, axis=0, keepdims=True)
            for v in range(variables):
                value = jnp.sum(hat * col_ref[v], axis=0, keepdims=True) * share
                rest = value - value.astype(jnp.bfloat16).astype(jnp.float32)
                highs[v][k] = jnp.where(in_b, value, 0.0).astype(jnp.bfloat16)
                lows[v][k] = jnp.where(in_b, rest, 0.0).astype(jnp.bfloat16)
        look = look_ref[e]
        acc_ref[...] += dot(look, jnp.concatenate(sum(highs, []), axis=0), last)
        acc2_ref[...] += dot(look[:KW], jnp.concatenate(sum(lows, []), axis=0), last)
        return carry

    lax.fori_loop(0, cells_ref.shape[0], entry, 0)
    by_b = acc_ref[:KW] + acc_ref[KW:] + acc2_ref[...]
    some = LANES // coarse_y
    wide = some * KW
    groups = by_b.shape[1] // LANES
    fetch.wait()
    tall = jnp.concatenate([taby_ref[...]] * some, axis=0)
    row, lane = rows_lanes(tall.shape)
    tall = jnp.where(row // coarse_y == lane // KW, tall, 0.0)
    stacked = jnp.concatenate([by_b[:, g * LANES : (g + 1) * LANES] for g in range(groups)], axis=0)
    target = dot(stacked, tall, precision=EXACT)
    for g in range(groups):
        at = pl.ds(g * wide, wide)
        d_ref[:, at] = p_ref[:, at] * scale - target[g * KW : (g + 1) * KW] * (RATIO * RATIO * scale)


def edge_kernel(after, f_ref, *refs):
    outs, buffer, sem = refs[:4], refs[4], refs[5]
    count, cells_x, cells_y = f_ref.shape
    row, lane = rows_lanes((cells_x, cells_y))
    copies = [pltpu.make_async_copy(buffer.at[i], outs[i], sem.at[i]) for i in range(4)]
    for i in range(count):
        buffer[0, i : i + 1, :] = f_ref[i, 0:1, :]
        buffer[1, i : i + 1, :] = f_ref[i, cells_x - 1 : cells_x, :]
    copies[0].start()
    copies[1].start()
    for side, at in ((2, 0), (3, cells_y - 1)):
        for i in range(count):
            edge = jnp.broadcast_to(f_ref[i, :, at : at + 1], (cells_x, cells_y))
            buffer[side, i : i + 1, :] = jnp.sum(
                jnp.where(row == lane, edge, 0.0), axis=0, keepdims=True
            )
        copies[side].start()
    for copy in copies:
        copy.wait()


def stencil_kernel(
    after, f_ref, terrain_ref, west_ref, east_ref, south_ref, north_ref, out_ref, *, variables
):
    count, cells_x, cells_y = f_ref.shape
    levels = count // variables
    row, lane = rows_lanes((cells_x, cells_y))
    south = jnp.transpose(south_ref[...])
    north = jnp.transpose(north_ref[...])
    metric = TOP / (TOP - terrain_ref[...].astype(jnp.float32))
    metric = metric * metric * 0.1
    for i in range(count):
        k = i % levels
        q = f_ref[i]
        wind_x = f_ref[k]
        wind_y = f_ref[levels + k]
        east = jnp.where(row == cells_x - 1, east_ref[i : i + 1, :], pltpu.roll(q, cells_x - 1, 0))
        west = jnp.where(row == 0, west_ref[i : i + 1, :], pltpu.roll(q, 1, 0))
        above = jnp.where(
            lane == cells_y - 1, north[:cells_x, i : i + 1], pltpu.roll(q, cells_y - 1, 1)
        )
        below = jnp.where(lane == 0, south[:cells_x, i : i + 1], pltpu.roll(q, 1, 1))
        transport = wind_x * (east - west) + wind_y * (above - below)
        diffusion = east + west + above + below - 4.0 * q
        upper = f_ref[i + 1] if k < levels - 1 else q
        lower = f_ref[i - 1] if k > 0 else q
        mixing = (upper - 2.0 * q + lower) * metric
        out_ref[i] = q - 0.05 * transport + 0.1 * diffusion + mixing


def nudge_kernel(
    state_ref, n_ref, bx_hbm, by_hbm, out_hbm, coeffs_ref, out_ref, bx_ref, by_ref, low_ref,
    out_sem, bx_sem, by_sem
):
    count, cells_x, cells_y = state_ref.shape
    per = LANES // KW
    groups = count // per
    bx_copy = pltpu.make_async_copy(bx_hbm.at[lax.axis_index("gx")], bx_ref, bx_sem)
    by_copy = pltpu.make_async_copy(by_hbm.at[lax.axis_index("gy")], by_ref, by_sem)
    bx_copy.start()
    by_copy.start()
    nudge = n_ref[...]
    high, low = split(nudge)
    bx_copy.wait()
    along = dot(bx_ref[...], jnp.concatenate([high, high, low], axis=0))
    high, low = split(along)
    left = jnp.concatenate(
        [
            jnp.concatenate([x[:, g * LANES : (g + 1) * LANES] for x in (high, low, high)], axis=1)
            for g in range(groups)
        ],
        axis=0,
    )
    by_copy.wait()
    by4 = by_ref[...].astype(jnp.float32)
    block, _ = rows_lanes(by4.shape)
    right = jnp.concatenate(
        [jnp.where(block % LANES // KW == q, by4, 0.0).astype(jnp.bfloat16) for q in range(per)],
        axis=1,
    )
    low_ref[...] = dot(left, right)
    copies = []
    for g in range(groups):
        for q in range(per):
            i = per * g + q
            out_ref[i] = state_ref[i] + low_ref[
                g * cells_x : (g + 1) * cells_x, q * cells_y : (q + 1) * cells_y
            ]
        at = pl.ds(per * g, per)
        copies.append(pltpu.make_async_copy(out_ref.at[at], out_hbm.at[at], out_sem.at[g]))
        copies[-1].start()
    for i in range(count):
        coeffs_ref[i] = nudge[:, i * KW : (i + 1) * KW]
    for copy in copies:
        copy.wait()


FAR = pl.BlockSpec(memory_space=pltpu.HBM)
LOOSE = pl.BlockSpec(memory_space=pl.ANY)
NEAR = pl.BlockSpec(memory_space=pltpu.VMEM)
DMA = pltpu.SemaphoreType.DMA


def call(kernel, ins, specs, outs, out_specs, scratch=()):
    return pl.pallas_call(
        kernel,
        out_shape=[jax.ShapeDtypeStruct(s, d) for s, d in outs],
        in_specs=specs,
        out_specs=out_specs,
        scratch_shapes=list(scratch),
        compiler_params=pltpu.CompilerParams(vmem_limit_bytes=48 << 20),
    )(
        *[
            pltpu.with_memory_space_constraint(x, pltpu.HBM) if spec is FAR else x
            for x, spec in zip(ins, specs)
        ]
    )


def gather(piece, axis):
    count = lax.axis_size(axis)
    return lax.all_to_all(
        jnp.broadcast_to(piece[None], (count,) + piece.shape), axis, 0, 0, tiled=True
    )


def shift(piece, axis, step):
    count = lax.axis_size(axis)
    return lax.ppermute(
        piece, axis, [(i, i + step) for i in range(count) if 0 <= i + step < count]
    )


def per_device(fields, terrain, columns, record_tile, record_cells, record_weights):
    tiles_x, tiles_y = lax.axis_size("gx"), lax.axis_size("gy")
    variables, levels, cells_x, cells_y = fields.shape
    total_x, total_y = cells_x * tiles_x, cells_y * tiles_y
    coarse_x, coarse_y = cells_x // RATIO, cells_y // RATIO
    count = variables * levels
    wide = count * KW
    parents, records = columns.shape[1:]
    entries = record_cells.shape[1]
    scale = 1.0 / np.sqrt(total_x * total_y)
    per = LANES // KW
    f32, b16 = jnp.float32, jnp.bfloat16

    wave_x, wave_y = wave_rows(total_x), wave_rows(total_y)
    by_x = wave_x.reshape(KW, tiles_x, cells_x).transpose(1, 0, 2)
    by_y = wave_y.reshape(KW, tiles_y, cells_y).transpose(1, 0, 2)
    tab_bx = two_parts(by_x, -2)
    tab_byt = two_parts(np.tile(by_y.transpose(0, 2, 1), (1, 1, per)), -1)
    tab_ax = two_parts(wave_x[:, ::RATIO], -2)
    tab_ay = np.tile(
        by_y[:, :, ::RATIO].transpose(0, 2, 1), (1, 1, LANES // coarse_y)
    ).astype(np.float32)
    tab_low_x = two_parts(-4.0 * scale * by_x.transpose(0, 2, 1), -1)
    tab_low_x = np.concatenate([tab_low_x, tab_low_x[..., :KW]], axis=-1)
    tab_low_y = two_parts(np.tile(by_y, (1, per, 1)), -2)
    tab_low_y = np.concatenate(
        [tab_low_y[:, :LANES], tab_low_y[:, :LANES], tab_low_y[:, LANES:]], axis=1
    )

    f = fields.reshape(count, cells_x, cells_y)
    coarse = coarse_x * coarse_y
    padded = -(-coarse // LANES) * LANES
    own = terrain[::RATIO, ::RATIO].astype(f32).reshape(coarse)
    own = jnp.pad(own, (0, padded - coarse)).reshape(padded // LANES, LANES)
    heights = gather(own, "gx").reshape(tiles_x, padded)

    tile, cells = record_tile.T, record_cells.T
    nest, look = call(
        functools.partial(ready_kernel, coarse_x=coarse_x, coarse_y=coarse_y),
        (f, tab_bx, tab_byt, tile, cells, tab_ax),
        [FAR] * 6,
        [((KW, wide), f32), ((entries, 2 * KW, records), b16)],
        [NEAR, NEAR],
        [
            pltpu.VMEM(f.shape, f32),
            pltpu.VMEM(tab_bx.shape[1:], b16),
            pltpu.VMEM(tab_byt.shape[1:], b16),
            pltpu.VMEM(tile.shape, jnp.int32),
            pltpu.VMEM(cells.shape, jnp.int32),
            pltpu.VMEM(tab_ax.shape, b16),
            DMA((count // per,)),
            DMA,
            DMA,
            DMA((3,)),
        ],
    )
    (part,) = call(
        functools.partial(record_kernel, levels=levels, coarse_y=coarse_y, scale=scale),
        (heights, tile, cells, record_weights.T.astype(f32), columns, look, nest, tab_ay),
        [NEAR] * 7 + [FAR],
        [((KW, wide), f32)],
        [NEAR],
        [
            pltpu.VMEM(columns.shape, f32),
            pltpu.VMEM((padded, records), f32),
            pltpu.VMEM((2 * KW, count * coarse_y), f32),
            pltpu.VMEM((KW, count * coarse_y), f32),
            pltpu.VMEM(tab_ay.shape[1:], f32),
            DMA,
        ],
    )
    x0, x1, y0, y1 = call(
        edge_kernel,
        (part, f),
        [LOOSE, NEAR],
        [((count, cells_y), f32)] * 4,
        [FAR] * 4,
        [pltpu.VMEM((4, count, cells_y), f32), DMA((4,))],
    )

    pieces = part.reshape(tiles_x, part.size // (tiles_x * LANES), LANES)
    mine = jnp.sum(lax.all_to_all(pieces, "gx", 0, 0, tiled=True), axis=0)
    west, east = shift(x1, "gx", 1), shift(x0, "gx", -1)
    mine, west, east, y0, y1 = lax.optimization_barrier((mine, west, east, y0, y1))
    south, north = shift(y1, "gy", 1), shift(y0, "gy", -1)
    mine = jnp.sum(gather(mine, "gy"), axis=0)
    mine, south, north = lax.optimization_barrier((mine, south, north))
    nudge = gather(mine, "gx").reshape(part.shape)

    (state,) = call(
        functools.partial(stencil_kernel, variables=variables),
        (mine, f, terrain, west, east, south, north),
        [LOOSE] + [NEAR] * 6,
        [(f.shape, f32)],
        [NEAR],
    )
    updated, coeffs = call(
        nudge_kernel,
        (state, nudge, tab_low_x, tab_low_y),
        [NEAR, NEAR, FAR, FAR],
        [(f.shape, f32), ((count, KW, KW), f32)],
        [FAR, NEAR],
        [
            pltpu.VMEM(f.shape, f32),
            pltpu.VMEM(tab_low_x.shape[1:], b16),
            pltpu.VMEM(tab_low_y.shape[1:], b16),
            pltpu.VMEM((count // per * cells_x, per * cells_y), f32),
            DMA((count // per,)),
            DMA,
            DMA,
        ],
    )
    return updated.reshape(fields.shape), coeffs.reshape(variables, levels, KW, KW)


def solution(mesh):
    return jax.shard_map(
        per_device,
        mesh=mesh,
        in_specs=(
            P(None, None, "gx", "gy"),
            P("gx", "gy"),
            P(None, None, ("gx", "gy")),
            P(("gx", "gy"), None),
            P(("gx", "gy"), None),
            P(("gx", "gy"), None),
        ),
        out_specs=(P(None, None, "gx", "gy"), P()),
        check_vma=False,
    )
```

time: 105 us -> 94.1 us (0.90)
  the two profiles are of different devices: /device:TPU:6 before, /device:TPU:1 now
where the time goes in v2:
time: 94.1 us; the launch traced here: 93.5 us
  starting transfers between devices  51.7 us (55%)
  waiting for transfers between devices  24.5 us (26%)
  Pallas kernels  12.1 us (13%)
  local copies, waits for them, and re-layouts  3.64 us (4%)
    all_to_all x3, starting transfers between devices, gather(): lax.all_to_all(jnp.broadcast_to(piece[None], (count,) + piece.shape), axi...  36.6 us
    all_to_all x3, waiting for transfers between devices, gather(): lax.all_to_all(jnp.broadcast_to(piece[None], (count,) + piece.shape), axi...  20.6 us
    pallas_call x5, Pallas kernels, call(): pl.pallas_call(kernel, out_shape=[jax.ShapeDtypeStruct(s, d) for s, d in...  12.1 us
    ppermute x4, starting transfers between devices, shift(): lax.ppermute(piece, axis, [(i, i + step) for i in range(count) if 0 <= i...  10.8 us
    all_to_all x1, starting transfers between devices, per_device(): mine = jnp.sum(lax.all_to_all(pieces, 'gx', 0, 0, tiled=True), axis=0)  4.24 us
    all_to_all x1, waiting for transfers between devices, per_device(): mine = jnp.sum(lax.all_to_all(pieces, 'gx', 0, 0, tiled=True), axis=0)  3.25 us
    broadcast_in_dim x4, local copies, waits for them, and re-layouts, gather(): jnp.broadcast_to(piece[None], (count,) + piece.shape)  1.95 us
  transfers between devices with their start and end apart: 8, of which 5 were waited for; matrix products, arithmetic and copies ran while one was open for 1% of the time, Pallas kernels for 6%

profile of v2, /device:TPU:1, one launch (start us, length us, event | category | flops | bytes accessed | tf_op | source)
XLA Modules:
  0.0 93.5 jit_solution(9290264197869050227)
XLA Ops:
  0.6 0.9 slice.3
  1.6 0.6 broadcast_in_dim.9
  2.3 14.0 %all-to-all-start = ((f32[32,2,128]{2,1,0:T(2,128)}), f32[32,2,128]{2,1,0:T(2,128)S(1)}, u32[]{:S(2)}, u32[]{:S(2)}) async-start(f32[32,2,128]{2,1,0:T(2,128)} %broadcast_in_dim.9), calls=%async_computation | async-start | bytes 65536 | tf_op jit(solution)/shard_map/all_to_all | solution.py:296
  16.3 0.7 convert_bitcast_fusion.weights_ref
  17.0 3.2 %shard_map.131 = (f32[32,768]{1,0:T(8,128)S(1)}, bf16[4,64,384]{2,1,0:T(8,128)(2,1)S(1)}) custom-call(f32[24,96,128]{2,1,0:T(8,128)} %bitcast.17, bf16[32,64,96]{2,1,0:T(8,128)(2,1)} %constant.16.clone.bx_hbm, bf16[24,128,256]{2,1,0:T(8,128)(2,1)} %constant.17.clone.by_hbm, s32[1,384]{1,0:T(1,128)} %bitcast.24, s32[4,384]{1,0:T(4,128)} %bitcast.22, ...), custom_call_target="tpu_custom_call" | custom-call | tf_op jit(solution)/shard_map/pallas_call | solution.py:279
  20.2 5.8 %all-to-all-done = f32[32,2,128]{2,1,0:T(2,128)S(1)} async-done(((f32[32,2,128]{2,1,0:T(2,128)}), f32[32,2,128]{2,1,0:T(2,128)S(1)}, u32[]{:S(2)}, u32[]{:S(2)}) %all-to-all-start) | async-done | bytes 32800 | tf_op jit(solution)/shard_map/all_to_all | solution.py:296
  26.1 3.4 %shard_map.132.after = f32[32,768]{1,0:T(8,128)S(1)} custom-call(f32[32,256]{1,0:T(8,128)S(1)} %bitcast.21, s32[1,384]{1,0:T(1,128)S(1)} %bitcast.25, s32[4,384]{1,0:T(4,128)S(1)} %bitcast.23, f32[4,384]{1,0:T(4,128)S(1)} %convert_bitcast_fusion.weights_ref, bf16[3,60,384]{2,1,0:T(8,128)(2,1)S(1)} %copy-done.1, ...), custom_call_target="tpu_custom_call" | custom-call | tf_op jit(solution)/shard_map/pallas_call | solution.py:279
  29.5 0.7 reshape.31
  30.2 4.2 %all-to-all-start.1 = ((f32[32,6,128]{2,1,0:T(8,128)}), f32[32,6,128]{2,1,0:T(8,128)S(1)}, u32[]{:S(2)}, u32[]{:S(2)}) async-start(f32[32,6,128]{2,1,0:T(8,128)} %reshape.31), calls=%async_computation.1 | async-start | bytes 262144 | tf_op jit(solution)/shard_map/all_to_all | solution.py:389
  34.4 0.9 shard_map.133
  35.3 4.4 %collective-permute-start = (f32[24,128]{1,0:T(8,128)S(1)}, f32[24,128]{1,0:T(8,128)S(1)}, u32[]{:S(2)}, u32[]{:S(2)}) collective-permute-start(f32[24,128]{1,0:T(8,128)S(1)} %get-tuple-element.20), channel_id=1, source_target_pairs={{0,24},{24,48},{48,72},{72,96},{96,120},{120,144},{144,168},{168,1... | collective-permute-start | bytes 36872 | tf_op jit(solution)/shard_map/ppermute | solution.py:303
  39.7 1.9 %collective-permute-start.1 = (f32[24,128]{1,0:T(8,128)S(1)}, f32[24,128]{1,0:T(8,128)S(1)}, u32[]{:S(2)}, u32[]{:S(2)}) collective-permute-start(f32[24,128]{1,0:T(8,128)S(1)} %get-tuple-element.21), channel_id=1, source_target_pairs={{24,0},{48,24},{72,48},{96,72},{120,96},{144,120},{168,144},{192,1... | collective-permute-start | bytes 36872 | tf_op jit(solution)/shard_map/ppermute | solution.py:303
  41.6 3.3 %all-to-all-done.1 = f32[32,6,128]{2,1,0:T(8,128)S(1)} async-done(((f32[32,6,128]{2,1,0:T(8,128)}), f32[32,6,128]{2,1,0:T(8,128)S(1)}, u32[]{:S(2)}, u32[]{:S(2)}) %all-to-all-start.1) | async-done | bytes 98336 | tf_op jit(solution)/shard_map/all_to_all | solution.py:389
  44.9 0.7 collective-permute-done.1.east_ref
  45.6 0.6 broadcast_in_dim.10
  46.3 12.4 %all-to-all-start.2 = ((f32[24,6,128]{2,1,0:T(8,128)}), f32[24,6,128]{2,1,0:T(8,128)S(1)}, u32[]{:S(2)}, u32[]{:S(2)}) async-start(f32[24,6,128]{2,1,0:T(8,128)} %broadcast_in_dim.10), calls=%async_computation.2 | async-start | bytes 196608 | tf_op jit(solution)/shard_map/all_to_all | solution.py:296
  58.7 3.2 %collective-permute-start.2 = (f32[24,128]{1,0:T(8,128)S(1)}, f32[24,128]{1,0:T(8,128)S(1)}, u32[]{:S(2)}, u32[]{:S(2)}) collective-permute-start(f32[24,128]{1,0:T(8,128)S(1)} %get-tuple-element.25), channel_id=1, source_target_pairs={{0,1},{1,2},{2,3},{3,4},{4,5},{5,6},{6,7},{7,8},{8,9},{9,10},{10,1... | collective-permute-start | bytes 36872 | tf_op jit(solution)/shard_map/ppermute | solution.py:303
  61.9 1.3 %collective-permute-start.3 = (f32[24,128]{1,0:T(8,128)S(1)}, f32[24,128]{1,0:T(8,128)S(1)}, u32[]{:S(2)}, u32[]{:S(2)}) collective-permute-start(f32[24,128]{1,0:T(8,128)S(1)} %get-tuple-element.26), channel_id=1, source_target_pairs={{1,0},{2,1},{3,2},{4,3},{5,4},{6,5},{7,6},{8,7},{9,8},{10,9},{11,1... | collective-permute-start | bytes 36872 | tf_op jit(solution)/shard_map/ppermute | solution.py:303
  63.2 5.3 %all-to-all-done.2 = f32[24,6,128]{2,1,0:T(8,128)S(1)} async-done(((f32[24,6,128]{2,1,0:T(8,128)}), f32[24,6,128]{2,1,0:T(8,128)S(1)}, u32[]{:S(2)}, u32[]{:S(2)}) %all-to-all-start.2) | async-done | bytes 73760 | tf_op jit(solution)/shard_map/all_to_all | solution.py:296
  68.5 0.7 broadcast_in_dim.22
  69.2 10.2 %all-to-all-start.3 = ((f32[32,6,128]{2,1,0:T(8,128)}), f32[32,6,128]{2,1,0:T(8,128)S(1)}, u32[]{:S(2)}, u32[]{:S(2)}) async-start(f32[32,6,128]{2,1,0:T(8,128)} %broadcast_in_dim.22), calls=%async_computation.3 | async-start | bytes 262144 | tf_op jit(solution)/shard_map/all_to_all | solution.py:296
  79.4 1.5 %shard_map.134.state_ref = f32[24,96,128]{2,1,0:T(8,128)S(1)} custom-call(f32[6,128]{1,0:T(8,128)S(1)} %reduce_sum.19.after, f32[24,96,128]{2,1,0:T(8,128)S(1)} %bitcast.19, s32[96,128]{1,0:T(8,128)S(1)} %copy-done.2, f32[24,128]{1,0:T(8,128)S(1)} %collective-permute-done.west_ref, f32[24,128]{1,0:T(8,128)S(1)} %collective-permute-done.1.east_ref, ...), custom_call_target="tpu_custom_call" | custom-call | tf_op jit(solution)/shard_map/pallas_call | solution.py:279
  80.9 9.5 %all-to-all-done.3 = f32[32,6,128]{2,1,0:T(8,128)S(1)} async-done(((f32[32,6,128]{2,1,0:T(8,128)}), f32[32,6,128]{2,1,0:T(8,128)S(1)}, u32[]{:S(2)}, u32[]{:S(2)}) %all-to-all-start.3) | async-done | bytes 98336 | tf_op jit(solution)/shard_map/all_to_all | solution.py:296
  90.4 3.1 %shard_map.135 = (f32[24,96,128]{2,1,0:T(8,128)}, f32[24,32,32]{2,1,0:T(8,128)}) custom-call(f32[24,96,128]{2,1,0:T(8,128)S(1)} %shard_map.134.state_ref, f32[32,768]{1,0:T(8,128)S(1)} %bitcast.20, bf16[32,96,96]{2,1,0:T(8,128)(2,1)} %constant.20.clone.bx_hbm, bf16[24,384,128]{2,1,0:T(8,128)(2,1)} %constant.21.clone.by_hbm), custom_call_target="tpu_custom_call" | custom-call | tf_op jit(solution)/shard_map/pallas_call | solution.py:279
  (20 shorter events, 0.2 us)
Async XLA Ops:
  2.3 23.8 %all-to-all-start = ((f32[32,2,128]{2,1,0:T(2,128)}), f32[32,2,128]{2,1,0:T(2,128)S(1)}, u32[]{:S(2)}, u32[]{:S(2)}) async-start(f32[32,2,128]{2,1,0:T(2,128)} %broadcast_in_dim.9), calls=%async_computation | async-start | bytes 65536 | tf_op jit(solution)/shard_map/all_to_all | solution.py:296
  17.0 9.1 %copy-start.1 = (bf16[3,60,384]{2,1,0:T(8,128)(2,1)S(1)}, bf16[3,60,384]{2,1,0:T(8,128)(2,1)}, u32[]{:S(2)}) copy-start(bf16[3,60,384]{2,1,0:T(8,128)(2,1)} %cols_ref.1) | copy-start | bytes 414724
  17.0 9.1 %copy-start.3 = (s32[384,4]{0,1:T(4,128)S(1)}, s32[384,4]{0,1:T(4,128)}, u32[]{:S(2)}) copy-start(s32[384,4]{0,1:T(4,128)} %param.16) | copy-start | bytes 18436
  17.0 9.1 %copy-start.4 = (s32[384,1]{0,1:T(1,128)S(1)}, s32[384,1]{0,1:T(1,128)}, u32[]{:S(2)}) copy-start(s32[384,1]{0,1:T(1,128)} %param.15) | copy-start | bytes 4612
  20.2 14.2 %copy-start = (f32[3,8,96,128]{3,2,1,0:T(8,128)S(1)}, f32[3,8,96,128]{3,2,1,0:T(8,128)}, u32[]{:S(2)}) copy-start(f32[3,8,96,128]{3,2,1,0:T(8,128)} %param.12) | copy-start | bytes 3538948
  30.2 49.2 %copy-start.2 = (s32[96,128]{1,0:T(8,128)S(1)}, s32[96,128]{1,0:T(8,128)}, u32[]{:S(2)}) copy-start(s32[96,128]{1,0:T(8,128)} %terrain_ref.1) | copy-start | bytes 147460
  30.2 14.8 %all-to-all-start.1 = ((f32[32,6,128]{2,1,0:T(8,128)}), f32[32,6,128]{2,1,0:T(8,128)S(1)}, u32[]{:S(2)}, u32[]{:S(2)}) async-start(f32[32,6,128]{2,1,0:T(8,128)} %reshape.31), calls=%async_computation.1 | async-start | bytes 262144 | tf_op jit(solution)/shard_map/all_to_all | solution.py:389
  35.3 9.7 %collective-permute-start = (f32[24,128]{1,0:T(8,128)S(1)}, f32[24,128]{1,0:T(8,128)S(1)}, u32[]{:S(2)}, u32[]{:S(2)}) collective-permute-start(f32[24,128]{1,0:T(8,128)S(1)} %get-tuple-element.20), channel_id=1, source_target_pairs={{0,24},{24,48},{48,72},{72,96},{96,120},{120,144},{144,168},{168,1... | collective-permute-start | bytes 36872 | tf_op jit(solution)/shard_map/ppermute | solution.py:303
  39.7 5.9 %collective-permute-start.1 = (f32[24,128]{1,0:T(8,128)S(1)}, f32[24,128]{1,0:T(8,128)S(1)}, u32[]{:S(2)}, u32[]{:S(2)}) collective-permute-start(f32[24,128]{1,0:T(8,128)S(1)} %get-tuple-element.21), channel_id=1, source_target_pairs={{24,0},{48,24},{72,48},{96,72},{120,96},{144,120},{168,144},{192,1... | collective-permute-start | bytes 36872 | tf_op jit(solution)/shard_map/ppermute | solution.py:303
  46.3 22.2 %all-to-all-start.2 = ((f32[24,6,128]{2,1,0:T(8,128)}), f32[24,6,128]{2,1,0:T(8,128)S(1)}, u32[]{:S(2)}, u32[]{:S(2)}) async-start(f32[24,6,128]{2,1,0:T(8,128)} %broadcast_in_dim.10), calls=%async_computation.2 | async-start | bytes 196608 | tf_op jit(solution)/shard_map/all_to_all | solution.py:296
  58.7 9.8 %collective-permute-start.2 = (f32[24,128]{1,0:T(8,128)S(1)}, f32[24,128]{1,0:T(8,128)S(1)}, u32[]{:S(2)}, u32[]{:S(2)}) collective-permute-start(f32[24,128]{1,0:T(8,128)S(1)} %get-tuple-element.25), channel_id=1, source_target_pairs={{0,1},{1,2},{2,3},{3,4},{4,5},{5,6},{6,7},{7,8},{8,9},{9,10},{10,1... | collective-permute-start | bytes 36872 | tf_op jit(solution)/shard_map/ppermute | solution.py:303
  61.9 6.6 %collective-permute-start.3 = (f32[24,128]{1,0:T(8,128)S(1)}, f32[24,128]{1,0:T(8,128)S(1)}, u32[]{:S(2)}, u32[]{:S(2)}) collective-permute-start(f32[24,128]{1,0:T(8,128)S(1)} %get-tuple-element.26), channel_id=1, source_target_pairs={{1,0},{2,1},{3,2},{4,3},{5,4},{6,5},{7,6},{8,7},{9,8},{10,9},{11,1... | collective-permute-start | bytes 36872 | tf_op jit(solution)/shard_map/ppermute | solution.py:303
  69.2 21.2 %all-to-all-start.3 = ((f32[32,6,128]{2,1,0:T(8,128)}), f32[32,6,128]{2,1,0:T(8,128)S(1)}, u32[]{:S(2)}, u32[]{:S(2)}) async-start(f32[32,6,128]{2,1,0:T(8,128)} %broadcast_in_dim.22), calls=%async_computation.3 | async-start | bytes 262144 | tf_op jit(solution)/shard_map/all_to_all | solution.py:296

commit v3 on v2

v3 whole, which is shorter than its diff:
```python
import functools

import jax
import jax.numpy as jnp
import numpy as np
from jax import lax
from jax.experimental import pallas as pl
from jax.experimental.pallas import tpu as pltpu
from jax.sharding import PartitionSpec as P

KW = 32
RATIO = 8
TOP = 12000.0
HIGHEST_CELL = 2999.0
LANES = 128
EXACT = lax.Precision.HIGHEST


def wave_rows(length):
    half = KW // 2
    x = np.arange(length)
    rows = [np.ones(length)]
    for m in range(1, half):
        rows.append(np.sqrt(2.0) * np.cos(2.0 * np.pi * (m * x % length) / length))
    for m in range(half, KW):
        rows.append(np.sqrt(2.0) * np.sin(2.0 * np.pi * ((m - half + 1) * x % length) / length))
    return np.stack(rows)


def turns(outer, inner, length):
    half = KW // 2
    wave = np.arange(KW)
    wave = np.where(wave < half, wave, wave - half + 1)[:, None]
    a = 2.0 * np.pi * (wave * outer[None, :] % length) / length
    c = 2.0 * np.pi * (wave * inner[None, :] % length) / length
    size = np.where(wave == 0, 1.0, np.sqrt(2.0))
    cosine = np.arange(KW)[:, None] < half
    with_cos = size * np.where(cosine, np.cos(a), np.sin(a))
    with_sin = size * np.where(cosine, -np.sin(a), np.cos(a))
    return np.concatenate([with_cos, with_sin]), np.concatenate([np.cos(c), np.sin(c)])


def two_parts(table, axis):
    whole = table.astype(np.float32)
    high = whole.astype(jnp.bfloat16)
    low = (whole - high.astype(np.float32)).astype(jnp.bfloat16)
    return np.concatenate([high, low], axis=axis)


def dot(a, b, dims=((1,), (0,)), precision=None):
    return lax.dot_general(
        a, b, (dims, ((), ())), precision=precision, preferred_element_type=jnp.float32
    )


def rows_lanes(shape):
    return (
        lax.broadcasted_iota(jnp.int32, shape, 0),
        lax.broadcasted_iota(jnp.int32, shape, 1),
    )


def split(x):
    high = x.astype(jnp.bfloat16)
    return high, (x - high.astype(jnp.float32)).astype(jnp.bfloat16)


def by_parity(axis, a, b):
    first = lax.rem(lax.axis_index(axis), 2) == 0
    return jnp.where(first, a, b), jnp.where(first, b, a)


def hot(mask):
    return jnp.where(mask, 1.0, 0.0).astype(jnp.bfloat16)


def ready_kernel(
    f_hbm, bx_hbm, by_hbm, tile_hbm, cells_hbm, taba_hbm, tabc_hbm, p_ref, look_ref,
    xa_ref, xb_ref, ya_ref, yb_ref, f_ref, bx_ref, by_ref, tile_ref, cells_ref, taba_ref, tabc_ref, f_sem, bx_sem, by_sem, small_sem,
    *, coarse_y
):
    count, cells_x, cells_y = f_ref.shape
    per = LANES // KW
    groups = count // per
    fetch = pltpu.make_async_copy(f_hbm, f_ref, f_sem)
    by_copy = pltpu.make_async_copy(by_hbm.at[lax.axis_index("gy")], by_ref, by_sem)
    bx_copy = pltpu.make_async_copy(bx_hbm.at[lax.axis_index("gx")], bx_ref, bx_sem)
    small = [
        pltpu.make_async_copy(a, b, small_sem.at[i])
        for i, (a, b) in enumerate(
            (
                (tile_hbm, tile_ref),
                (cells_hbm, cells_ref),
                (taba_hbm, taba_ref),
                (tabc_hbm, tabc_ref),
            )
        )
    ]
    for copy in (*small, by_copy, fetch, bx_copy):
        copy.start()
    for copy in small:
        copy.wait()
    records = tile_ref.shape[1]
    row_t, _ = rows_lanes((taba_ref.shape[1], records))
    row_c, _ = rows_lanes((tabc_ref.shape[1], records))
    both = dot(taba_ref[...], hot(row_t == tile_ref[...]))
    outer = both[: 2 * KW] + both[2 * KW :]
    cells = cells_ref[...] // coarse_y
    for e in range(cells_ref.shape[0]):
        both = dot(tabc_ref[...], hot(row_c == cells[e : e + 1, :]))
        inner = both[: 2 * KW] + both[2 * KW :]
        turned = outer * inner
        high, low = split(turned[:KW] + turned[KW:])
        look_ref[:KW, e * records : (e + 1) * records] = high
        look_ref[KW:, e * records : (e + 1) * records] = low
    by_copy.wait()
    by4 = by_ref[...].astype(jnp.float32)
    _, lane = rows_lanes(by4.shape)
    spread = jnp.concatenate(
        [
            jnp.where(lane % LANES // KW == q, by4, 0.0).astype(jnp.bfloat16)
            for q in range(per)
        ],
        axis=0,
    )
    fetch.wait()
    bx_copy.wait()
    values = jnp.concatenate(
        [
            jnp.concatenate([f_ref[per * g + q] for q in range(per)], axis=1)
            for g in range(groups)
        ],
        axis=0,
    )
    high, low = split(values)
    both = dot(high, spread)
    along = both[:, :LANES] + both[:, LANES:] + dot(low, spread[:, :LANES])
    high, low = split(
        jnp.concatenate([along[g * cells_x : (g + 1) * cells_x] for g in range(groups)], axis=1)
    )
    both = dot(bx_ref[...], high)
    p_ref[...] = both[:KW] + both[KW:] + dot(bx_ref[:KW, :], low)
    row, lane = rows_lanes((cells_x, cells_y))
    for i in range(count):
        for ref, at in ((xa_ref, cells_x - 1), (xb_ref, 0)):
            ref[i : i + 1, :] = f_ref[i, at : at + 1, :]
        for ref, at in ((ya_ref, cells_y - 1), (yb_ref, 0)):
            edge = jnp.broadcast_to(f_ref[i, :, at : at + 1], (cells_x, cells_y))
            ref[i : i + 1, :] = jnp.sum(jnp.where(row == lane, edge, 0.0), axis=0, keepdims=True)
    for axis, a_ref, b_ref in (("gx", xa_ref, xb_ref), ("gy", ya_ref, yb_ref)):
        a_ref[...], b_ref[...] = by_parity(axis, a_ref[...], b_ref[...])


def reach(k, levels, parents, highest):
    bottoms = [h + (k - 0.5) * (TOP - h) / levels for h in (0.0, highest)]
    tops = [h + (k + 1.5) * (TOP - h) / levels for h in (0.0, highest)]
    step = TOP / parents
    first = int(np.floor((min(bottoms) - 1.0) / step - 0.5))
    last = int(np.ceil((max(tops) + 1.0) / step - 0.5)) + 1
    return max(0, first) // 8 * 8, min(-(-parents // 8), -(-last // 8)) * 8


def record_kernel(
    h_ref, tile_ref, cells_ref, weights_ref, cols_ref, look_ref, p_ref, taby_hbm, d_ref,
    col_ref, pick_ref, high_ref, low_ref, taby_ref, sem, *, levels, coarse_y, scale
):
    variables, parents, records = cols_ref.shape
    tiles, padded = h_ref.shape
    count = variables * levels
    fetch = pltpu.make_async_copy(taby_hbm.at[lax.axis_index("gy")], taby_ref, sem)
    fetch.start()
    tile = tile_ref[...]
    row, _ = rows_lanes((tiles, records))
    tile_hot = hot(row == tile)
    heights = h_ref[...]
    high = jnp.floor(heights * (1.0 / 64.0))
    low = heights - 64.0 * high
    over = ((0,), (0,))
    pick_ref[...] = 64.0 * dot(high.astype(jnp.bfloat16), tile_hot, over) + dot(
        low.astype(jnp.bfloat16), tile_hot, over
    )
    col_ref[...] = jnp.zeros_like(col_ref)
    for v in range(variables):
        col_ref[v, :parents, :] = cols_ref[v].astype(jnp.float32)
    row_c, _ = rows_lanes((padded, records))
    row_b, _ = rows_lanes((coarse_y, records))
    row_p, _ = rows_lanes(col_ref.shape[1:])
    parent = jnp.where(row_p < parents, (row_p.astype(jnp.float32) + 0.5) * (TOP / parents), 1e9)
    cells = cells_ref[...]
    weights = weights_ref[...].astype(jnp.float32)
    for e in range(cells_ref.shape[0]):
        at = slice(e * records, (e + 1) * records)
        cell = cells[e : e + 1, :]
        height = jnp.sum(jnp.where(row_c == cell, pick_ref[...], 0.0), axis=0, keepdims=True)
        in_b = row_b == cell % coarse_y
        inverse = levels / (TOP - height)
        shift_k = height * inverse + 0.5
        apart = parent * inverse - shift_k
        for k in range(levels):
            first, last = reach(k, levels, parents, HIGHEST_CELL)
            hat = jnp.maximum(0.0, 1.0 - jnp.abs(apart[first:last] - float(k)))
            share = weights[e : e + 1, :] / jnp.sum(hat, axis=0, keepdims=True)
            for v in range(variables):
                value = jnp.sum(hat * col_ref[v, first:last, :], axis=0, keepdims=True) * share
                rest = value - value.astype(jnp.bfloat16).astype(jnp.float32)
                i = (v * levels + k) * coarse_y
                high_ref[i : i + coarse_y, at] = jnp.where(in_b, value, 0.0).astype(jnp.bfloat16)
                low_ref[i : i + coarse_y, at] = jnp.where(in_b, rest, 0.0).astype(jnp.bfloat16)
    last = ((1,), (1,))
    both = dot(high_ref[...], look_ref[...], last)
    by_b = both[:, :KW] + both[:, KW:] + dot(low_ref[...], look_ref[:KW, :], last)
    some = LANES // coarse_y
    groups = count // some
    fetch.wait()
    tall = jnp.concatenate([taby_ref[...]] * some, axis=0)
    row, lane = rows_lanes(tall.shape)
    tall = jnp.where(row // coarse_y == lane // KW, tall, 0.0)
    for g in range(groups):
        target = dot(by_b[g * LANES : (g + 1) * LANES], tall, over, precision=EXACT)
        for i in range(some * KW // LANES):
            j = g * (some * KW // LANES) + i
            here = slice(j * LANES, (j + 1) * LANES)
            part = p_ref[:, here] * scale - target[:, i * LANES : (i + 1) * LANES] * (
                RATIO * RATIO * scale
            )
            for m in range(KW // 8):
                d_ref[:, m * p_ref.shape[1] // LANES + j, :] = part[8 * m : 8 * m + 8]


def stencil_kernel(
    after, f_ref, terrain_ref, xa_ref, xb_ref, ya_ref, yb_ref, out_ref, east_ref, west_ref,
    *, variables
):
    count, cells_x, cells_y = f_ref.shape
    levels = count // variables
    row, lane = rows_lanes((cells_x, cells_y))
    east_ref[...], west_ref[...] = by_parity("gx", xa_ref[...], xb_ref[...])
    north, south = by_parity("gy", ya_ref[...], yb_ref[...])
    south = jnp.transpose(south)
    north = jnp.transpose(north)
    metric = TOP / (TOP - terrain_ref[...].astype(jnp.float32))
    metric = metric * metric * 0.1
    for i in range(count):
        k = i % levels
        q = f_ref[i]
        wind_x = f_ref[k]
        wind_y = f_ref[levels + k]
        east = jnp.where(row == cells_x - 1, east_ref[i : i + 1, :], pltpu.roll(q, cells_x - 1, 0))
        west = jnp.where(row == 0, west_ref[i : i + 1, :], pltpu.roll(q, 1, 0))
        above = jnp.where(
            lane == cells_y - 1, north[:cells_x, i : i + 1], pltpu.roll(q, cells_y - 1, 1)
        )
        below = jnp.where(lane == 0, south[:cells_x, i : i + 1], pltpu.roll(q, 1, 1))
        transport = wind_x * (east - west) + wind_y * (above - below)
        diffusion = east + west + above + below - 4.0 * q
        upper = f_ref[i + 1] if k < levels - 1 else q
        lower = f_ref[i - 1] if k > 0 else q
        mixing = (upper - 2.0 * q + lower) * metric
        out_ref[i] = q - 0.05 * transport + 0.1 * diffusion + mixing


def nudge_kernel(
    state_ref, n_ref, bx_hbm, by_hbm, out_hbm, coeffs_hbm, out_ref, coeffs_ref, bx_ref, by_ref,
    low_ref, out_sem, coeffs_sem, bx_sem, by_sem
):
    count, cells_x, cells_y = state_ref.shape
    per = LANES // KW
    groups = count // per
    bx_copy = pltpu.make_async_copy(bx_hbm.at[lax.axis_index("gx")], bx_ref, bx_sem)
    by_copy = pltpu.make_async_copy(by_hbm.at[lax.axis_index("gy")], by_ref, by_sem)
    bx_copy.start()
    by_copy.start()
    nudge = jnp.concatenate(
        [
            jnp.concatenate([n_ref[:, m * groups + g, :] for m in range(KW // 8)], axis=0)
            for g in range(groups)
        ],
        axis=1,
    )
    high, low = split(nudge)
    bx_copy.wait()
    along = dot(bx_ref[...], jnp.concatenate([high, high, low], axis=0))
    high, low = split(along)
    by_copy.wait()
    by4 = by_ref[...].astype(jnp.float32)
    block, _ = rows_lanes(by4.shape)
    right = jnp.concatenate(
        [jnp.where(block % LANES // KW == q, by4, 0.0).astype(jnp.bfloat16) for q in range(per)],
        axis=1,
    )
    for i in range(count):
        coeffs_ref[i] = nudge[:, i * KW : (i + 1) * KW]
    copies = [pltpu.make_async_copy(coeffs_ref, coeffs_hbm, coeffs_sem)]
    copies[0].start()
    halves = 2
    some = groups // halves
    for half in range(halves):
        left = jnp.concatenate(
            [
                jnp.concatenate([x[:, g * LANES : (g + 1) * LANES] for x in (high, low, high)], axis=1)
                for g in range(half * some, (half + 1) * some)
            ],
            axis=0,
        )
        low_ref[...] = dot(left, right)
        for g in range(some):
            for q in range(per):
                i = per * (half * some + g) + q
                out_ref[i] = state_ref[i] + low_ref[
                    g * cells_x : (g + 1) * cells_x, q * cells_y : (q + 1) * cells_y
                ]
            at = pl.ds(per * (half * some + g), per)
            copies.append(
                pltpu.make_async_copy(out_ref.at[at], out_hbm.at[at], out_sem.at[half * some + g])
            )
            copies[-1].start()
    for copy in copies:
        copy.wait()


FAR = pl.BlockSpec(memory_space=pltpu.HBM)
LOOSE = pl.BlockSpec(memory_space=pl.ANY)
NEAR = pl.BlockSpec(memory_space=pltpu.VMEM)
DMA = pltpu.SemaphoreType.DMA


def call(kernel, ins, specs, outs, out_specs, scratch=()):
    return pl.pallas_call(
        kernel,
        out_shape=[jax.ShapeDtypeStruct(s, d) for s, d in outs],
        in_specs=specs,
        out_specs=out_specs,
        scratch_shapes=list(scratch),
        compiler_params=pltpu.CompilerParams(vmem_limit_bytes=48 << 20),
    )(
        *[
            pltpu.with_memory_space_constraint(x, pltpu.HBM) if spec is FAR else x
            for x, spec in zip(ins, specs)
        ]
    )


def gather(piece, axis, groups=None):
    count = len(groups[0]) if groups else lax.axis_size(axis)
    return lax.all_to_all(
        jnp.broadcast_to(piece[None], (count,) + piece.shape),
        axis, 0, 0, axis_index_groups=groups, tiled=True,
    )


def near_groups(tiles_x, tiles_y):
    every = np.arange(tiles_x * tiles_y).reshape(-1, 4, 2, tiles_y // 2, 2)
    along_gx = np.arange(tiles_x).reshape(-1, 4, 2)
    wide = along_gx.transpose(1, 0, 2).reshape(4, -1)
    tall = every.transpose(0, 2, 3, 1, 4).reshape(-1, 8)
    deep = np.arange(tiles_y).reshape(-1, 2).T
    return wide.tolist(), tall.tolist(), deep.tolist()


def swap(piece, axis, start):
    pairs = [(i, i + 1) for i in range(start, lax.axis_size(axis) - 1, 2)]
    return lax.ppermute(piece, axis, pairs + [(j, i) for i, j in pairs])


def per_device(fields, terrain, columns, record_tile, record_cells, record_weights):
    tiles_x, tiles_y = lax.axis_size("gx"), lax.axis_size("gy")
    variables, levels, cells_x, cells_y = fields.shape
    total_x, total_y = cells_x * tiles_x, cells_y * tiles_y
    coarse_x, coarse_y = cells_x // RATIO, cells_y // RATIO
    count = variables * levels
    wide = count * KW
    parents, records = columns.shape[1:]
    entries = record_cells.shape[1]
    scale = 1.0 / np.sqrt(total_x * total_y)
    per = LANES // KW
    f32, b16 = jnp.float32, jnp.bfloat16

    wave_x, wave_y = wave_rows(total_x), wave_rows(total_y)
    by_x = wave_x.reshape(KW, tiles_x, cells_x).transpose(1, 0, 2)
    by_y = wave_y.reshape(KW, tiles_y, cells_y).transpose(1, 0, 2)
    tab_bx = two_parts(by_x, -2)
    tab_byt = two_parts(np.tile(by_y.transpose(0, 2, 1), (1, 1, per)), -1)
    outer, inner = turns(cells_x * np.arange(tiles_x), RATIO * np.arange(coarse_x), total_x)
    tab_a = two_parts(outer, -2)
    tab_c = two_parts(np.pad(inner, ((0, 0), (0, -coarse_x % 16))), -2)
    tab_ay = np.tile(
        by_y[:, :, ::RATIO].transpose(0, 2, 1), (1, 1, LANES // coarse_y)
    ).astype(np.float32)
    tab_low_x = two_parts(-4.0 * scale * by_x.transpose(0, 2, 1), -1)
    tab_low_x = np.concatenate([tab_low_x, tab_low_x[..., :KW]], axis=-1)
    tab_low_y = two_parts(np.tile(by_y, (1, per, 1)), -2)
    tab_low_y = np.concatenate(
        [tab_low_y[:, :LANES], tab_low_y[:, :LANES], tab_low_y[:, LANES:]], axis=1
    )

    f = fields.reshape(count, cells_x, cells_y)
    coarse = coarse_x * coarse_y
    padded = -(-coarse // LANES) * LANES
    own = terrain[::RATIO, ::RATIO].astype(f32).reshape(coarse)
    own = jnp.pad(own, (0, padded - coarse)).reshape(padded // LANES, LANES)
    heights = gather(own, "gx").reshape(tiles_x, padded)

    tile, cells = record_tile.T, record_cells.T
    nest, look, xa, xb, ya, yb = call(
        functools.partial(ready_kernel, coarse_y=coarse_y),
        (f, tab_bx, tab_byt, tile, cells, tab_a, tab_c),
        [FAR] * 7,
        [((KW, wide), f32), ((2 * KW, entries * records), b16)] + [((count, cells_y), f32)] * 4,
        [NEAR] * 6,
        [
            pltpu.VMEM(f.shape, f32),
            pltpu.VMEM(tab_bx.shape[1:], b16),
            pltpu.VMEM(tab_byt.shape[1:], b16),
            pltpu.VMEM(tile.shape, jnp.int32),
            pltpu.VMEM(cells.shape, jnp.int32),
            pltpu.VMEM(tab_a.shape, b16),
            pltpu.VMEM(tab_c.shape, b16),
            DMA,
            DMA,
            DMA,
            DMA((4,)),
        ],
    )
    (part,) = call(
        functools.partial(record_kernel, levels=levels, coarse_y=coarse_y, scale=scale),
        (heights, tile, cells, record_weights.T, columns, look, nest, tab_ay),
        [NEAR] * 7 + [FAR],
        [((8, KW // 8 * wide // LANES, LANES), f32)],
        [NEAR],
        [
            pltpu.VMEM((variables, -(-parents // 8) * 8, records), f32),
            pltpu.VMEM((padded, records), f32),
            pltpu.VMEM((count * coarse_y, entries * records), b16),
            pltpu.VMEM((count * coarse_y, entries * records), b16),
            pltpu.VMEM(tab_ay.shape[1:], f32),
            DMA,
        ],
    )
    wide_groups, tall_groups, deep_groups = near_groups(tiles_x, tiles_y)
    pieces = part.reshape(len(wide_groups[0]), -1, LANES)
    mine = jnp.sum(
        lax.all_to_all(pieces, "gx", 0, 0, axis_index_groups=wide_groups, tiled=True).reshape(
            pieces.shape
        ),
        axis=0,
    )
    xa, xb, ya, yb, _ = lax.optimization_barrier((xa, xb, ya, yb, part))
    xa = swap(xa, "gx", 0)
    mine, xa, xb, ya, yb = lax.optimization_barrier((mine, xa, xb, ya, yb))
    xb = swap(xb, "gx", 1)
    mine = jnp.sum(gather(mine, ("gx", "gy"), tall_groups), axis=0)
    mine, xb, ya, yb = lax.optimization_barrier((mine, xb, ya, yb))
    yb, ya = swap(yb, "gy", 1), swap(ya, "gy", 0)
    mine = jnp.sum(gather(mine, "gy", deep_groups), axis=0)
    mine, ya, yb = lax.optimization_barrier((mine, ya, yb))
    nudge = gather(mine, "gx", wide_groups).reshape(part.shape)

    (state,) = call(
        functools.partial(stencil_kernel, variables=variables),
        (mine, f, terrain, xa, xb, ya, yb),
        [LOOSE] + [NEAR] * 6,
        [(f.shape, f32)],
        [NEAR],
        [pltpu.VMEM(xa.shape, f32)] * 2,
    )
    updated, coeffs = call(
        nudge_kernel,
        (state, nudge, tab_low_x, tab_low_y),
        [NEAR, NEAR, FAR, FAR],
        [(f.shape, f32), ((count, KW, KW), f32)],
        [FAR, FAR],
        [
            pltpu.VMEM(f.shape, f32),
            pltpu.VMEM((count, KW, KW), f32),
            pltpu.VMEM(tab_low_x.shape[1:], b16),
            pltpu.VMEM(tab_low_y.shape[1:], b16),
            pltpu.VMEM((count // per // 2 * cells_x, per * cells_y), f32),
            DMA((count // per,)),
            DMA,
            DMA,
            DMA,
        ],
    )
    return updated.reshape(fields.shape), coeffs.reshape(variables, levels, KW, KW)


def solution(mesh):
    return jax.shard_map(
        per_device,
        mesh=mesh,
        in_specs=(
            P(None, None, "gx", "gy"),
            P("gx", "gy"),
            P(None, None, ("gx", "gy")),
            P(("gx", "gy"), None),
            P(("gx", "gy"), None),
            P(("gx", "gy"), None),
        ),
        out_specs=(P(None, None, "gx", "gy"), P()),
        check_vma=False,
    )
```

time: 94.1 us -> 88.5 us (0.940)
  Pallas kernels: 12.1 us -> 9.52 us
  starting transfers between devices: 51.7 us -> 50.2 us
    pallas_call x5 -> x4, Pallas kernels: 12.1 us -> 9.52 us  [call(): pl.pallas_call(kernel, out_shape=[jax.ShapeDtypeStruct(s, d) for s, d in...]
    broadcast_in_dim x4 -> x5, local copies, waits for them, and re-layouts: 1.95 us -> 2.61 us  [gather(): jnp.broadcast_to(piece[None], (count,) + piece.shape)]
    all_to_all x3 -> x4, starting transfers between devices: 36.6 us -> 36.1 us  [gather(): lax.all_to_all(jnp.broadcast_to(piece[None], (count,) + piece.shape), axi...]
    all_to_all x3 -> x4, waiting for transfers between devices: 20.6 us -> 20.6 us  [gather(): lax.all_to_all(jnp.broadcast_to(piece[None], (count,) + piece.shape), axi...]
  transfers between devices with their start and end apart: 8 -> 9, of which waited for: 5 -> 5; matrix products, arithmetic and copies ran while one was open for 1% -> 0% of each run, Pallas kernels for 6% -> 4%
where the time goes in v3:
time: 88.5 us; the launch traced here: 87.8 us
  starting transfers between devices  50.2 us (57%)
  waiting for transfers between devices  23.6 us (27%)
  Pallas kernels  9.52 us (11%)
  local copies, waits for them, and re-layouts  3.62 us (4%)
    all_to_all x4, starting transfers between devices, gather(): lax.all_to_all(jnp.broadcast_to(piece[None], (count,) + piece.shape), axi...  36.1 us
    all_to_all x4, waiting for transfers between devices, gather(): lax.all_to_all(jnp.broadcast_to(piece[None], (count,) + piece.shape), axi...  20.6 us
    ppermute x4, starting transfers between devices, swap(): return lax.ppermute(piece, axis, pairs + [(j, i) for i, j in pairs])  10.4 us
    pallas_call x4, Pallas kernels, call(): pl.pallas_call(kernel, out_shape=[jax.ShapeDtypeStruct(s, d) for s, d in...  9.52 us
    all_to_all x1, starting transfers between devices, per_device(): lax.all_to_all(pieces, 'gx', 0, 0, axis_index_groups=wide_groups, tiled=T...  3.67 us
    all_to_all x1, waiting for transfers between devices, per_device(): lax.all_to_all(pieces, 'gx', 0, 0, axis_index_groups=wide_groups, tiled=T...  2.98 us
    broadcast_in_dim x5, local copies, waits for them, and re-layouts, gather(): jnp.broadcast_to(piece[None], (count,) + piece.shape)  2.61 us
  transfers between devices with their start and end apart: 9, of which 5 were waited for; matrix products, arithmetic and copies ran while one was open for 0% of the time, Pallas kernels for 4%

profile of v3, /device:TPU:1, one launch (start us, length us, event | category | flops | bytes accessed | tf_op | source)
XLA Modules:
  0.0 87.8 jit_solution(9111909673511719424)
XLA Ops:
  0.6 0.9 %slice.3 = s32[12,16]{1,0:T(8,128)S(1)} slice(s32[96,128]{1,0:T(8,128)} %terrain_ref.1), slice={[0:96:8], [0:128:8]} | slice | bytes 1536 | tf_op jit(solution)/shard_map/slice | solution.py:399
  1.5 0.1 reshape.23
  1.6 0.6 broadcast_in_dim.11
  2.3 14.0 %all-to-all-start = ((f32[32,2,128]{2,1,0:T(2,128)}), f32[32,2,128]{2,1,0:T(2,128)S(1)}, u32[]{:S(2)}, u32[]{:S(2)}) async-start(f32[32,2,128]{2,1,0:T(2,128)} %broadcast_in_dim.11), calls=%async_computation | async-start | bytes 65536 | tf_op jit(solution)/shard_map/all_to_all | solution.py:345
  16.3 2.3 %shard_map.140 = (f32[32,768]{1,0:T(8,128)S(1)}, bf16[64,1536]{1,0:T(8,128)(2,1)S(1)}, f32[24,128]{1,0:T(8,128)S(1)}, f32[24,128]{1,0:T(8,128)S(1)}, f32[24,128]{1,0:T(8,128)S(1)}, /*index=5*/f32[24,128]{1,0:T(8,128)S(1)}) custom-call(f32[24,96,128]{2,1,0:T(8,128)} %bitcast.12, bf16[32,64,96]{2,1,0:T(8,128)(2,1)} %constant.18.clone.bx_hbm, ...), custom_call_target="tpu_custom_call" | custom-call | tf_op jit(solution)/shard_map/pallas_call | solution.py:328
  18.7 7.4 %all-to-all-done = f32[32,2,128]{2,1,0:T(2,128)S(1)} async-done(((f32[32,2,128]{2,1,0:T(2,128)}), f32[32,2,128]{2,1,0:T(2,128)S(1)}, u32[]{:S(2)}, u32[]{:S(2)}) %all-to-all-start) | async-done | bytes 32800 | tf_op jit(solution)/shard_map/all_to_all | solution.py:345
  26.1 3.3 %shard_map.141 = f32[8,24,128]{2,1,0:T(8,128)} custom-call(f32[32,256]{1,0:T(8,128)S(1)} %bitcast.14, s32[1,384]{1,0:T(1,128)S(1)} %bitcast.18, s32[4,384]{1,0:T(4,128)S(1)} %bitcast.16, bf16[4,384]{1,0:T(4,128)(2,1)S(1)} %bitcast.19, bf16[3,60,384]{2,1,0:T(8,128)(2,1)S(1)} %copy-done.1, bf16[64,1536]{1,0:T(8,128)(2,1)S(1)} %get-tuple-element.26.look_ref, ...), custom_call_target="tpu_custom_call" | custom-call | tf_op jit(solution)/shard_map/pallas_call | solution.py:328
  29.4 3.7 %all-to-all-start.1 = ((f32[8,24,128]{2,1,0:T(8,128)}), f32[8,24,128]{2,1,0:T(8,128)S(1)}, u32[]{:S(2)}, u32[]{:S(2)}) async-start(f32[8,24,128]{2,1,0:T(8,128)} %shard_map.141), calls=%async_computation.1 | async-start | bytes 196608 | tf_op jit(solution)/shard_map/all_to_all | solution.py:442
  33.1 2.0 %collective-permute-start = (f32[24,128]{1,0:T(8,128)S(1)}, f32[24,128]{1,0:T(8,128)S(1)}, u32[]{:S(2)}, u32[]{:S(2)}) collective-permute-start(f32[24,128]{1,0:T(8,128)S(1)} %get-tuple-element.32), channel_id=1, source_target_pairs={{0,24},{48,72},{96,120},{144,168},{192,216},{240,264},{288,312},{3... | collective-permute-start | bytes 36872 | tf_op jit(solution)/shard_map/ppermute | solution.py:362
  35.1 3.0 %all-to-all-done.1 = f32[8,24,128]{2,1,0:T(8,128)S(1)} async-done(((f32[8,24,128]{2,1,0:T(8,128)}), f32[8,24,128]{2,1,0:T(8,128)S(1)}, u32[]{:S(2)}, u32[]{:S(2)}) %all-to-all-start.1) | async-done | bytes 98336 | tf_op jit(solution)/shard_map/all_to_all | solution.py:442
  38.1 0.6 broadcast_in_dim.12
  38.7 3.4 %all-to-all-start.2 = ((f32[8,24,128]{2,1,0:T(8,128)}), f32[8,24,128]{2,1,0:T(8,128)S(1)}, u32[]{:S(2)}, u32[]{:S(2)}) async-start(f32[8,24,128]{2,1,0:T(8,128)} %broadcast_in_dim.12), calls=%async_computation.2 | async-start | bytes 196608 | tf_op jit(solution)/shard_map/all_to_all | solution.py:345
  42.1 5.1 %collective-permute-start.1 = (f32[24,128]{1,0:T(8,128)S(1)}, f32[24,128]{1,0:T(8,128)S(1)}, u32[]{:S(2)}, u32[]{:S(2)}) collective-permute-start(f32[24,128]{1,0:T(8,128)S(1)} %get-tuple-element.37), channel_id=1, source_target_pairs={{24,48},{72,96},{120,144},{168,192},{216,240},{264,288},{312,336},... | collective-permute-start | bytes 36872 | tf_op jit(solution)/shard_map/ppermute | solution.py:362
  47.3 2.2 %all-to-all-done.2 = f32[8,24,128]{2,1,0:T(8,128)S(1)} async-done(((f32[8,24,128]{2,1,0:T(8,128)}), f32[8,24,128]{2,1,0:T(8,128)S(1)}, u32[]{:S(2)}, u32[]{:S(2)}) %all-to-all-start.2) | async-done | bytes 98336 | tf_op jit(solution)/shard_map/all_to_all | solution.py:345
  49.5 0.7 broadcast_in_dim.13
  50.2 12.0 %all-to-all-start.3 = ((f32[12,24,128]{2,1,0:T(8,128)}), f32[12,24,128]{2,1,0:T(8,128)S(1)}, u32[]{:S(2)}, u32[]{:S(2)}) async-start(f32[12,24,128]{2,1,0:T(8,128)} %broadcast_in_dim.13), calls=%async_computation.3 | async-start | bytes 294912 | tf_op jit(solution)/shard_map/all_to_all | solution.py:345
  62.2 2.6 %collective-permute-start.2 = (f32[24,128]{1,0:T(8,128)S(1)}, f32[24,128]{1,0:T(8,128)S(1)}, u32[]{:S(2)}, u32[]{:S(2)}) collective-permute-start(f32[24,128]{1,0:T(8,128)S(1)} %get-tuple-element.41), channel_id=1, source_target_pairs={{0,1},{2,3},{4,5},{6,7},{8,9},{10,11},{12,13},{14,15},{16,17},{18,... | collective-permute-start | bytes 36872 | tf_op jit(solution)/shard_map/ppermute | solution.py:362
  64.7 0.7 collective-permute-start.3
  65.4 7.5 %all-to-all-done.3 = f32[12,24,128]{2,1,0:T(8,128)S(1)} async-done(((f32[12,24,128]{2,1,0:T(8,128)}), f32[12,24,128]{2,1,0:T(8,128)S(1)}, u32[]{:S(2)}, u32[]{:S(2)}) %all-to-all-start.3) | async-done | bytes 147488 | tf_op jit(solution)/shard_map/all_to_all | solution.py:345
  72.9 0.6 broadcast_in_dim.14
  73.6 6.8 %all-to-all-start.4 = ((f32[8,24,128]{2,1,0:T(8,128)}), f32[8,24,128]{2,1,0:T(8,128)S(1)}, u32[]{:S(2)}, u32[]{:S(2)}) async-start(f32[8,24,128]{2,1,0:T(8,128)} %broadcast_in_dim.14), calls=%async_computation.4 | async-start | bytes 196608 | tf_op jit(solution)/shard_map/all_to_all | solution.py:345
  80.4 1.5 %shard_map.142.state_ref = f32[24,96,128]{2,1,0:T(8,128)S(1)} custom-call(f32[24,128]{1,0:T(8,128)S(1)} %reduce_sum.29.after, f32[24,96,128]{2,1,0:T(8,128)S(1)} %bitcast.13, s32[96,128]{1,0:T(8,128)S(1)} %copy-done.2, f32[24,128]{1,0:T(8,128)S(1)} %collective-permute-done.xa_ref, f32[24,128]{1,0:T(8,128)S(1)} %collective-permute-done.1.xb_ref, ...), custom_call_target="tpu_custom_call" | custom-call | tf_op jit(solution)/shard_map/pallas_call | solution.py:328
  81.9 3.5 %all-to-all-done.4.n_ref = f32[8,24,128]{2,1,0:T(8,128)S(1)} async-done(((f32[8,24,128]{2,1,0:T(8,128)}), f32[8,24,128]{2,1,0:T(8,128)S(1)}, u32[]{:S(2)}, u32[]{:S(2)}) %all-to-all-start.4) | async-done | bytes 98336 | tf_op jit(solution)/shard_map/all_to_all | solution.py:345
  85.4 2.4 %shard_map.143 = (f32[24,96,128]{2,1,0:T(8,128)}, f32[24,32,32]{2,1,0:T(8,128)}) custom-call(f32[24,96,128]{2,1,0:T(8,128)S(1)} %shard_map.142.state_ref, f32[8,24,128]{2,1,0:T(8,128)S(1)} %all-to-all-done.4.n_ref, bf16[32,96,96]{2,1,0:T(8,128)(2,1)} %constant.23.clone.bx_hbm, bf16[24,384,128]{2,1,0:T(8,128)(2,1)} %constant.24.clone.by_hbm), custom_call_target="tpu_custom_call" | custom-call | tf_op jit(solution)/shard_map/pallas_call | solution.py:328
  (22 shorter events, 0.1 us)
Async XLA Ops:
  2.3 23.8 %all-to-all-start = ((f32[32,2,128]{2,1,0:T(2,128)}), f32[32,2,128]{2,1,0:T(2,128)S(1)}, u32[]{:S(2)}, u32[]{:S(2)}) async-start(f32[32,2,128]{2,1,0:T(2,128)} %broadcast_in_dim.11), calls=%async_computation | async-start | bytes 65536 | tf_op jit(solution)/shard_map/all_to_all | solution.py:345
  16.3 9.8 %copy-start.1 = (bf16[3,60,384]{2,1,0:T(8,128)(2,1)S(1)}, bf16[3,60,384]{2,1,0:T(8,128)(2,1)}, u32[]{:S(2)}) copy-start(bf16[3,60,384]{2,1,0:T(8,128)(2,1)} %cols_ref.1) | copy-start | bytes 414724
  16.3 9.8 %copy-start.3 = (s32[384,4]{0,1:T(4,128)S(1)}, s32[384,4]{0,1:T(4,128)}, u32[]{:S(2)}) copy-start(s32[384,4]{0,1:T(4,128)} %param.17) | copy-start | bytes 18436
  16.3 9.8 %copy-start.4 = (s32[384,1]{0,1:T(1,128)S(1)}, s32[384,1]{0,1:T(1,128)}, u32[]{:S(2)}) copy-start(s32[384,1]{0,1:T(1,128)} %param.16) | copy-start | bytes 4612
  16.3 9.8 %copy-start.5 = (bf16[384,4]{0,1:T(4,128)(2,1)S(1)}, bf16[384,4]{0,1:T(4,128)(2,1)}, u32[]{:S(2)}) copy-start(bf16[384,4]{0,1:T(4,128)(2,1)} %param.18) | copy-start | bytes 9220
  26.1 54.3 %copy-start = (f32[3,8,96,128]{3,2,1,0:T(8,128)S(1)}, f32[3,8,96,128]{3,2,1,0:T(8,128)}, u32[]{:S(2)}) copy-start(f32[3,8,96,128]{3,2,1,0:T(8,128)} %param.13) | copy-start | bytes 3538948
  26.1 54.3 %copy-start.2 = (s32[96,128]{1,0:T(8,128)S(1)}, s32[96,128]{1,0:T(8,128)}, u32[]{:S(2)}) copy-start(s32[96,128]{1,0:T(8,128)} %terrain_ref.1) | copy-start | bytes 147460
  29.4 8.7 %all-to-all-start.1 = ((f32[8,24,128]{2,1,0:T(8,128)}), f32[8,24,128]{2,1,0:T(8,128)S(1)}, u32[]{:S(2)}, u32[]{:S(2)}) async-start(f32[8,24,128]{2,1,0:T(8,128)} %shard_map.141), calls=%async_computation.1 | async-start | bytes 196608 | tf_op jit(solution)/shard_map/all_to_all | solution.py:442
  33.1 5.0 %collective-permute-start = (f32[24,128]{1,0:T(8,128)S(1)}, f32[24,128]{1,0:T(8,128)S(1)}, u32[]{:S(2)}, u32[]{:S(2)}) collective-permute-start(f32[24,128]{1,0:T(8,128)S(1)} %get-tuple-element.32), channel_id=1, source_target_pairs={{0,24},{48,72},{96,120},{144,168},{192,216},{240,264},{288,312},{3... | collective-permute-start | bytes 36872 | tf_op jit(solution)/shard_map/ppermute | solution.py:362
  38.7 10.7 %all-to-all-start.2 = ((f32[8,24,128]{2,1,0:T(8,128)}), f32[8,24,128]{2,1,0:T(8,128)S(1)}, u32[]{:S(2)}, u32[]{:S(2)}) async-start(f32[8,24,128]{2,1,0:T(8,128)} %broadcast_in_dim.12), calls=%async_computation.2 | async-start | bytes 196608 | tf_op jit(solution)/shard_map/all_to_all | solution.py:345
  42.1 7.4 %collective-permute-start.1 = (f32[24,128]{1,0:T(8,128)S(1)}, f32[24,128]{1,0:T(8,128)S(1)}, u32[]{:S(2)}, u32[]{:S(2)}) collective-permute-start(f32[24,128]{1,0:T(8,128)S(1)} %get-tuple-element.37), channel_id=1, source_target_pairs={{24,48},{72,96},{120,144},{168,192},{216,240},{264,288},{312,336},... | collective-permute-start | bytes 36872 | tf_op jit(solution)/shard_map/ppermute | solution.py:362
  50.2 22.7 %all-to-all-start.3 = ((f32[12,24,128]{2,1,0:T(8,128)}), f32[12,24,128]{2,1,0:T(8,128)S(1)}, u32[]{:S(2)}, u32[]{:S(2)}) async-start(f32[12,24,128]{2,1,0:T(8,128)} %broadcast_in_dim.13), calls=%async_computation.3 | async-start | bytes 294912 | tf_op jit(solution)/shard_map/all_to_all | solution.py:345
  62.2 10.8 %collective-permute-start.2 = (f32[24,128]{1,0:T(8,128)S(1)}, f32[24,128]{1,0:T(8,128)S(1)}, u32[]{:S(2)}, u32[]{:S(2)}) collective-permute-start(f32[24,128]{1,0:T(8,128)S(1)} %get-tuple-element.41), channel_id=1, source_target_pairs={{0,1},{2,3},{4,5},{6,7},{8,9},{10,11},{12,13},{14,15},{16,17},{18,... | collective-permute-start | bytes 36872 | tf_op jit(solution)/shard_map/ppermute | solution.py:362
  64.7 8.2 %collective-permute-start.3 = (f32[24,128]{1,0:T(8,128)S(1)}, f32[24,128]{1,0:T(8,128)S(1)}, u32[]{:S(2)}, u32[]{:S(2)}) collective-permute-start(f32[24,128]{1,0:T(8,128)S(1)} %get-tuple-element.42), channel_id=1, source_target_pairs={{1,2},{3,4},{5,6},{7,8},{9,10},{11,12},{13,14},{15,16},{17,18},{19... | collective-permute-start | bytes 36872 | tf_op jit(solution)/shard_map/ppermute | solution.py:362
  73.6 11.8 %all-to-all-start.4 = ((f32[8,24,128]{2,1,0:T(8,128)}), f32[8,24,128]{2,1,0:T(8,128)S(1)}, u32[]{:S(2)}, u32[]{:S(2)}) async-start(f32[8,24,128]{2,1,0:T(8,128)} %broadcast_in_dim.14), calls=%async_computation.4 | async-start | bytes 196608 | tf_op jit(solution)/shard_map/all_to_all | solution.py:345

commit v4 on v3

--- a/solution.py
+++ b/solution.py
@@ -212,11 +212,19 @@
     some = LANES // coarse_y
     groups = count // some
     fetch.wait()
-    tall = jnp.concatenate([taby_ref[...]] * some, axis=0)
+    taby = taby_ref[...].astype(jnp.float32)
+    tall = jnp.concatenate([taby] * some, axis=0)
     row, lane = rows_lanes(tall.shape)
-    tall = jnp.where(row // coarse_y == lane // KW, tall, 0.0)
+    width = some * KW
+    tall = jnp.where(row // coarse_y == lane % width // KW, tall, 0.0).astype(jnp.bfloat16)
+    turned = jnp.concatenate(
+        [jnp.transpose(by_b[g * LANES : (g + 1) * LANES]) for g in range(groups)], axis=0
+    )
+    high, low = split(turned)
+    both = dot(high, tall)
+    targets = both[:, :width] + both[:, width:] + dot(low, tall[:, :width])
     for g in range(groups):
-        target = dot(by_b[g * LANES : (g + 1) * LANES], tall, over, precision=EXACT)
+        target = targets[g * KW : (g + 1) * KW]
         for i in range(some * KW // LANES):
             j = g * (some * KW // LANES) + i
             here = slice(j * LANES, (j + 1) * LANES)
@@ -228,9 +236,13 @@
 
 
 def stencil_kernel(
-    after, f_ref, terrain_ref, xa_ref, xb_ref, ya_ref, yb_ref, out_ref, east_ref, west_ref,
-    *, variables
+    after, f_ref, terrain_ref, xa_ref, xb_ref, ya_ref, yb_ref, bx_hbm, by_hbm, out_ref, bx_ref, right_ref,
+    east_ref, west_ref, by_ref, bx_sem, by_sem, *, variables
 ):
+    bx_copy = pltpu.make_async_copy(bx_hbm.at[lax.axis_index("gx")], bx_ref, bx_sem)
+    by_copy = pltpu.make_async_copy(by_hbm.at[lax.axis_index("gy")], by_ref, by_sem)
+    bx_copy.start()
+    by_copy.start()
     count, cells_x, cells_y = f_ref.shape
     levels = count // variables
     row, lane = rows_lanes((cells_x, cells_y))
@@ -257,19 +269,22 @@
         lower = f_ref[i - 1] if k > 0 else q
         mixing = (upper - 2.0 * q + lower) * metric
         out_ref[i] = q - 0.05 * transport + 0.1 * diffusion + mixing
+    by_copy.wait()
+    by4 = by_ref[...].astype(jnp.float32)
+    block, _ = rows_lanes(by4.shape)
+    for q in range(LANES // KW):
+        right_ref[:, q * cells_y : (q + 1) * cells_y] = jnp.where(
+            block % LANES // KW == q, by4, 0.0
+        ).astype(jnp.bfloat16)
+    bx_copy.wait()
 
 
 def nudge_kernel(
-    state_ref, n_ref, bx_hbm, by_hbm, out_hbm, coeffs_hbm, out_ref, coeffs_ref, bx_ref, by_ref,
-    low_ref, out_sem, coeffs_sem, bx_sem, by_sem
+    state_ref, n_ref, bx_ref, right_ref, out_hbm, coeffs_hbm, out_ref, coeffs_ref, low_ref, out_sem, coeffs_sem
 ):
     count, cells_x, cells_y = state_ref.shape
     per = LANES // KW
     groups = count // per
-    bx_copy = pltpu.make_async_copy(bx_hbm.at[lax.axis_index("gx")], bx_ref, bx_sem)
-    by_copy = pltpu.make_async_copy(by_hbm.at[lax.axis_index("gy")], by_ref, by_sem)
-    bx_copy.start()
-    by_copy.start()
     nudge = jnp.concatenate(
         [
             jnp.concatenate([n_ref[:, m * groups + g, :] for m in range(KW // 8)], axis=0)
@@ -278,40 +293,32 @@
         axis=1,
     )
     high, low = split(nudge)
-    bx_copy.wait()
     along = dot(bx_ref[...], jnp.concatenate([high, high, low], axis=0))
     high, low = split(along)
-    by_copy.wait()
-    by4 = by_ref[...].astype(jnp.float32)
-    block, _ = rows_lanes(by4.shape)
-    right = jnp.concatenate(
-        [jnp.where(block % LANES // KW == q, by4, 0.0).astype(jnp.bfloat16) for q in range(per)],
-        axis=1,
-    )
     for i in range(count):
         coeffs_ref[i] = nudge[:, i * KW : (i + 1) * KW]
     copies = [pltpu.make_async_copy(coeffs_ref, coeffs_hbm, coeffs_sem)]
     copies[0].start()
-    halves = 2
-    some = groups // halves
-    for half in range(halves):
+    thirds = 3
+    some = groups // thirds
+    for third in range(thirds):
         left = jnp.concatenate(
             [
                 jnp.concatenate([x[:, g * LANES : (g + 1) * LANES] for x in (high, low, high)], axis=1)
-                for g in range(half * some, (half + 1) * some)
+                for g in range(third * some, (third + 1) * some)
             ],
             axis=0,
         )
-        low_ref[...] = dot(left, right)
+        low_ref[...] = dot(left, right_ref[...])
         for g in range(some):
             for q in range(per):
-                i = per * (half * some + g) + q
+                i = per * (third * some + g) + q
                 out_ref[i] = state_ref[i] + low_ref[
                     g * cells_x : (g + 1) * cells_x, q * cells_y : (q + 1) * cells_y
                 ]
-            at = pl.ds(per * (half * some + g), per)
+            at = pl.ds(per * (third * some + g), per)
             copies.append(
-                pltpu.make_async_copy(out_ref.at[at], out_hbm.at[at], out_sem.at[half * some + g])
+                pltpu.make_async_copy(out_ref.at[at], out_hbm.at[at], out_sem.at[third * some + g])
             )
             copies[-1].start()
     for copy in copies:
@@ -383,9 +390,9 @@
     outer, inner = turns(cells_x * np.arange(tiles_x), RATIO * np.arange(coarse_x), total_x)
     tab_a = two_parts(outer, -2)
     tab_c = two_parts(np.pad(inner, ((0, 0), (0, -coarse_x % 16))), -2)
-    tab_ay = np.tile(
-        by_y[:, :, ::RATIO].transpose(0, 2, 1), (1, 1, LANES // coarse_y)
-    ).astype(np.float32)
+    tab_ay = two_parts(
+        np.tile(by_y[:, :, ::RATIO].transpose(0, 2, 1), (1, 1, LANES // coarse_y)), -1
+    )
     tab_low_x = two_parts(-4.0 * scale * by_x.transpose(0, 2, 1), -1)
     tab_low_x = np.concatenate([tab_low_x, tab_low_x[..., :KW]], axis=-1)
     tab_low_y = two_parts(np.tile(by_y, (1, per, 1)), -2)
@@ -432,7 +439,7 @@
             pltpu.VMEM((padded, records), f32),
             pltpu.VMEM((count * coarse_y, entries * records), b16),
             pltpu.VMEM((count * coarse_y, entries * records), b16),
-            pltpu.VMEM(tab_ay.shape[1:], f32),
+            pltpu.VMEM(tab_ay.shape[1:], b16),
             DMA,
         ],
     )
@@ -444,40 +451,38 @@
         ),
         axis=0,
     )
-    xa, xb, ya, yb, _ = lax.optimization_barrier((xa, xb, ya, yb, part))
-    xa = swap(xa, "gx", 0)
     mine, xa, xb, ya, yb = lax.optimization_barrier((mine, xa, xb, ya, yb))
-    xb = swap(xb, "gx", 1)
+    ya, xa = swap(ya, "gy", 0), swap(xa, "gx", 0)
     mine = jnp.sum(gather(mine, ("gx", "gy"), tall_groups), axis=0)
-    mine, xb, ya, yb = lax.optimization_barrier((mine, xb, ya, yb))
-    yb, ya = swap(yb, "gy", 1), swap(ya, "gy", 0)
+    mine, xa, xb, ya, yb = lax.optimization_barrier((mine, xa, xb, ya, yb))
+    xb, yb = swap(xb, "gx", 1), swap(yb, "gy", 1)
     mine = jnp.sum(gather(mine, "gy", deep_groups), axis=0)
-    mine, ya, yb = lax.optimization_barrier((mine, ya, yb))
+    mine, xb, yb = lax.optimization_barrier((mine, xb, yb))
     nudge = gather(mine, "gx", wide_groups).reshape(part.shape)
 
-    (state,) = call(
+    state, low_x, low_y = call(
         functools.partial(stencil_kernel, variables=variables),
-        (mine, f, terrain, xa, xb, ya, yb),
-        [LOOSE] + [NEAR] * 6,
-        [(f.shape, f32)],
-        [NEAR],
-        [pltpu.VMEM(xa.shape, f32)] * 2,
+        (mine, f, terrain, xa, xb, ya, yb, tab_low_x, tab_low_y),
+        [LOOSE] + [NEAR] * 6 + [FAR] * 2,
+        [
+            (f.shape, f32),
+            (tab_low_x.shape[1:], b16),
+            (tab_low_y.shape[1:2] + (per * cells_y,), b16),
+        ],
+        [NEAR] * 3,
+        [pltpu.VMEM(xa.shape, f32)] * 2 + [pltpu.VMEM(tab_low_y.shape[1:], b16), DMA, DMA],
     )
     updated, coeffs = call(
         nudge_kernel,
-        (state, nudge, tab_low_x, tab_low_y),
-        [NEAR, NEAR, FAR, FAR],
+        (state, nudge, low_x, low_y),
+        [NEAR] * 4,
         [(f.shape, f32), ((count, KW, KW), f32)],
         [FAR, FAR],
         [
             pltpu.VMEM(f.shape, f32),
             pltpu.VMEM((count, KW, KW), f32),
-            pltpu.VMEM(tab_low_x.shape[1:], b16),
-            pltpu.VMEM(tab_low_y.shape[1:], b16),
-            pltpu.VMEM((count // per // 2 * cells_x, per * cells_y), f32),
+            pltpu.VMEM((count // per // 3 * cells_x, per * cells_y), f32),
             DMA((count // per,)),
-            DMA,
-            DMA,
             DMA,
         ],
     )

time: 88.5 us -> 86.1 us (0.973)
  blocking collectives: 0 us -> 7.75 us
  waiting for transfers between devices: 23.6 us -> 16.9 us
  starting transfers between devices: 50.2 us -> 48.4 us
  Pallas kernels: 9.52 us -> 8.01 us
    all_to_all x0 -> x1, blocking collectives: none -> 7.75 us  [per_device(): lax.all_to_all(pieces, 'gx', 0, 0, axis_index_groups=wide_groups, tiled=T...]
    all_to_all x4, waiting for transfers between devices: 20.6 us -> 16.6 us  [gather(): lax.all_to_all(jnp.broadcast_to(piece[None], (count,) + piece.shape), axi...]
    all_to_all x1 -> x0, starting transfers between devices: 3.67 us -> none  [per_device(): lax.all_to_all(pieces, 'gx', 0, 0, axis_index_groups=wide_groups, tiled=T...]
    all_to_all x1 -> x0, waiting for transfers between devices: 2.98 us -> none  [per_device(): lax.all_to_all(pieces, 'gx', 0, 0, axis_index_groups=wide_groups, tiled=T...]
    ppermute x4, starting transfers between devices: 10.4 us -> 12.2 us  [swap(): return lax.ppermute(piece, axis, pairs + [(j, i) for i, j in pairs])]
    pallas_call x4, Pallas kernels: 9.52 us -> 8.01 us  [call(): pl.pallas_call(kernel, out_shape=[jax.ShapeDtypeStruct(s, d) for s, d in...]
  transfers between devices with their start and end apart: 9 -> 8, of which waited for: 5 -> 5; matrix products, arithmetic and copies ran while one was open for 0% -> 0% of each run, Pallas kernels for 4% -> 5%
where the time goes in v4:
time: 86.1 us; the launch traced here: 85.5 us
  starting transfers between devices  48.4 us (56%)
  waiting for transfers between devices  16.9 us (20%)
  Pallas kernels  8.01 us (9%)
  blocking collectives  7.75 us (9%)
  local copies, waits for them, and re-layouts  3.62 us (4%)
    all_to_all x4, starting transfers between devices, gather(): lax.all_to_all(jnp.broadcast_to(piece[None], (count,) + piece.shape), axi...  36.1 us
    all_to_all x4, waiting for transfers between devices, gather(): lax.all_to_all(jnp.broadcast_to(piece[None], (count,) + piece.shape), axi...  16.6 us
    ppermute x4, starting transfers between devices, swap(): return lax.ppermute(piece, axis, pairs + [(j, i) for i, j in pairs])  12.2 us
    pallas_call x4, Pallas kernels, call(): pl.pallas_call(kernel, out_shape=[jax.ShapeDtypeStruct(s, d) for s, d in...  8.01 us
    all_to_all x1, blocking collectives, per_device(): lax.all_to_all(pieces, 'gx', 0, 0, axis_index_groups=wide_groups, tiled=T...  7.75 us
    broadcast_in_dim x5, local copies, waits for them, and re-layouts, gather(): jnp.broadcast_to(piece[None], (count,) + piece.shape)  2.61 us
  transfers between devices with their start and end apart: 8, of which 5 were waited for; matrix products, arithmetic and copies ran while one was open for 0% of the time, Pallas kernels for 5%

profile of v4, /device:TPU:1, one launch (start us, length us, event | category | flops | bytes accessed | tf_op | source)
XLA Modules:
  0.0 85.5 jit_solution(15144312158309814192)
XLA Ops:
  0.6 0.9 %slice.3 = s32[12,16]{1,0:T(8,128)S(1)} slice(s32[96,128]{1,0:T(8,128)} %terrain_ref.1), slice={[0:96:8], [0:128:8]} | slice | bytes 1536 | tf_op jit(solution)/shard_map/slice | solution.py:406
  1.5 0.1 reshape.23
  1.6 0.6 broadcast_in_dim.11
  2.3 14.0 %all-to-all-start = ((f32[32,2,128]{2,1,0:T(2,128)}), f32[32,2,128]{2,1,0:T(2,128)S(1)}, u32[]{:S(2)}, u32[]{:S(2)}) async-start(f32[32,2,128]{2,1,0:T(2,128)} %broadcast_in_dim.11), calls=%async_computation | async-start | bytes 65536 | tf_op jit(solution)/shard_map/all_to_all | solution.py:352
  16.3 2.3 %shard_map.140 = (f32[32,768]{1,0:T(8,128)S(1)}, bf16[64,1536]{1,0:T(8,128)(2,1)S(1)}, f32[24,128]{1,0:T(8,128)S(1)}, f32[24,128]{1,0:T(8,128)S(1)}, f32[24,128]{1,0:T(8,128)S(1)}, /*index=5*/f32[24,128]{1,0:T(8,128)S(1)}) custom-call(f32[24,96,128]{2,1,0:T(8,128)} %bitcast.12, bf16[32,64,96]{2,1,0:T(8,128)(2,1)} %constant.18.clone.bx_hbm, ...), custom_call_target="tpu_custom_call" | custom-call | tf_op jit(solution)/shard_map/pallas_call | solution.py:335
  18.7 7.4 %all-to-all-done = f32[32,2,128]{2,1,0:T(2,128)S(1)} async-done(((f32[32,2,128]{2,1,0:T(2,128)}), f32[32,2,128]{2,1,0:T(2,128)S(1)}, u32[]{:S(2)}, u32[]{:S(2)}) %all-to-all-start) | async-done | bytes 32800 | tf_op jit(solution)/shard_map/all_to_all | solution.py:352
  26.1 2.5 %shard_map.141 = f32[8,24,128]{2,1,0:T(8,128)S(1)} custom-call(f32[32,256]{1,0:T(8,128)S(1)} %bitcast.14, s32[1,384]{1,0:T(1,128)S(1)} %bitcast.18, s32[4,384]{1,0:T(4,128)S(1)} %bitcast.16, bf16[4,384]{1,0:T(4,128)(2,1)S(1)} %bitcast.19, bf16[3,60,384]{2,1,0:T(8,128)(2,1)S(1)} %copy-done.1, bf16[64,1536]{1,0:T(8,128)(2,1)S(1)} %get-tuple-element.26.look_ref, ...), custom_call_target="tpu_custom_call" | custom-call | tf_op jit(solution)/shard_map/pallas_call | solution.py:335
  28.6 7.8 %all_to_all.25 = f32[8,24,128]{2,1,0:T(8,128)S(1)} all-to-all(f32[8,24,128]{2,1,0:T(8,128)S(1)} %shard_map.141), channel_id=1, replica_groups={{0,24,192,216,384,408,576,600},{48,72,240,264,432,456,624,648},{96,120,..., dimensions={0} | all-to-all | bytes 196608 | tf_op jit(solution)/shard_map/all_to_all | solution.py:449
  36.4 0.6 broadcast_in_dim.12
  37.1 3.4 %all-to-all-start.2 = ((f32[8,24,128]{2,1,0:T(8,128)}), f32[8,24,128]{2,1,0:T(8,128)S(1)}, u32[]{:S(2)}, u32[]{:S(2)}) async-start(f32[8,24,128]{2,1,0:T(8,128)} %broadcast_in_dim.12), calls=%async_computation.2 | async-start | bytes 196608 | tf_op jit(solution)/shard_map/all_to_all | solution.py:352
  40.4 2.7 %collective-permute-start = (f32[24,128]{1,0:T(8,128)S(1)}, f32[24,128]{1,0:T(8,128)S(1)}, u32[]{:S(2)}, u32[]{:S(2)}) collective-permute-start(f32[24,128]{1,0:T(8,128)S(1)} %get-tuple-element.33), channel_id=1, source_target_pairs={{0,24},{48,72},{96,120},{144,168},{192,216},{240,264},{288,312},{3... | collective-permute-start | bytes 36872 | tf_op jit(solution)/shard_map/ppermute | solution.py:369
  43.2 3.5 %collective-permute-start.1 = (f32[24,128]{1,0:T(8,128)S(1)}, f32[24,128]{1,0:T(8,128)S(1)}, u32[]{:S(2)}, u32[]{:S(2)}) collective-permute-start(f32[24,128]{1,0:T(8,128)S(1)} %get-tuple-element.35), channel_id=1, source_target_pairs={{0,1},{2,3},{4,5},{6,7},{8,9},{10,11},{12,13},{14,15},{16,17},{18,... | collective-permute-start | bytes 36872 | tf_op jit(solution)/shard_map/ppermute | solution.py:369
  46.7 1.1 %all-to-all-done.2 = f32[8,24,128]{2,1,0:T(8,128)S(1)} async-done(((f32[8,24,128]{2,1,0:T(8,128)}), f32[8,24,128]{2,1,0:T(8,128)S(1)}, u32[]{:S(2)}, u32[]{:S(2)}) %all-to-all-start.2) | async-done | bytes 98336 | tf_op jit(solution)/shard_map/all_to_all | solution.py:352
  47.8 0.3 collective-permute-done.1.ya_ref
  48.1 0.7 broadcast_in_dim.13
  48.7 12.0 %all-to-all-start.3 = ((f32[12,24,128]{2,1,0:T(8,128)}), f32[12,24,128]{2,1,0:T(8,128)S(1)}, u32[]{:S(2)}, u32[]{:S(2)}) async-start(f32[12,24,128]{2,1,0:T(8,128)} %broadcast_in_dim.13), calls=%async_computation.3 | async-start | bytes 294912 | tf_op jit(solution)/shard_map/all_to_all | solution.py:352
  60.7 5.3 %collective-permute-start.2 = (f32[24,128]{1,0:T(8,128)S(1)}, f32[24,128]{1,0:T(8,128)S(1)}, u32[]{:S(2)}, u32[]{:S(2)}) collective-permute-start(f32[24,128]{1,0:T(8,128)S(1)} %get-tuple-element.38), channel_id=1, source_target_pairs={{24,48},{72,96},{120,144},{168,192},{216,240},{264,288},{312,336},... | collective-permute-start | bytes 36872 | tf_op jit(solution)/shard_map/ppermute | solution.py:369
  66.0 0.7 collective-permute-start.3
  66.7 4.8 %all-to-all-done.3 = f32[12,24,128]{2,1,0:T(8,128)S(1)} async-done(((f32[12,24,128]{2,1,0:T(8,128)}), f32[12,24,128]{2,1,0:T(8,128)S(1)}, u32[]{:S(2)}, u32[]{:S(2)}) %all-to-all-start.3) | async-done | bytes 147488 | tf_op jit(solution)/shard_map/all_to_all | solution.py:352
  71.5 0.6 broadcast_in_dim.14
  72.2 6.8 %all-to-all-start.4 = ((f32[8,24,128]{2,1,0:T(8,128)}), f32[8,24,128]{2,1,0:T(8,128)S(1)}, u32[]{:S(2)}, u32[]{:S(2)}) async-start(f32[8,24,128]{2,1,0:T(8,128)} %broadcast_in_dim.14), calls=%async_computation.4 | async-start | bytes 196608 | tf_op jit(solution)/shard_map/all_to_all | solution.py:352
  78.9 1.6 %shard_map.142 = (f32[24,96,128]{2,1,0:T(8,128)S(1)}, bf16[96,96]{1,0:T(8,128)(2,1)S(1)}, bf16[384,512]{1,0:T(8,128)(2,1)S(1)}) custom-call(f32[24,128]{1,0:T(8,128)S(1)} %reduce_sum.29.after, f32[24,96,128]{2,1,0:T(8,128)S(1)} %bitcast.13, s32[96,128]{1,0:T(8,128)S(1)} %copy-done.2, f32[24,128]{1,0:T(8,128)S(1)} %collective-permute-done.xa_ref, ...), custom_call_target="tpu_custom_call" | custom-call | tf_op jit(solution)/shard_map/pallas_call | solution.py:335
  80.6 3.4 %all-to-all-done.4.n_ref = f32[8,24,128]{2,1,0:T(8,128)S(1)} async-done(((f32[8,24,128]{2,1,0:T(8,128)}), f32[8,24,128]{2,1,0:T(8,128)S(1)}, u32[]{:S(2)}, u32[]{:S(2)}) %all-to-all-start.4) | async-done | bytes 98336 | tf_op jit(solution)/shard_map/all_to_all | solution.py:352
  83.9 1.6 %shard_map.143 = (f32[24,96,128]{2,1,0:T(8,128)}, f32[24,32,32]{2,1,0:T(8,128)}) custom-call(f32[24,96,128]{2,1,0:T(8,128)S(1)} %get-tuple-element.45.state_ref, f32[8,24,128]{2,1,0:T(8,128)S(1)} %all-to-all-done.4.n_ref, bf16[96,96]{1,0:T(8,128)(2,1)S(1)} %get-tuple-element.46.bx_ref, bf16[384,512]{1,0:T(8,128)(2,1)S(1)} %get-tuple-element.47.right_ref), custom_call_target="tpu_custom_call" | custom-call | tf_op jit(solution)/shard_map/pallas_call | solution.py:335
  (21 shorter events, 0.1 us)
Async XLA Ops:
  2.3 23.8 %all-to-all-start = ((f32[32,2,128]{2,1,0:T(2,128)}), f32[32,2,128]{2,1,0:T(2,128)S(1)}, u32[]{:S(2)}, u32[]{:S(2)}) async-start(f32[32,2,128]{2,1,0:T(2,128)} %broadcast_in_dim.11), calls=%async_computation | async-start | bytes 65536 | tf_op jit(solution)/shard_map/all_to_all | solution.py:352
  16.3 9.8 %copy-start.1 = (bf16[3,60,384]{2,1,0:T(8,128)(2,1)S(1)}, bf16[3,60,384]{2,1,0:T(8,128)(2,1)}, u32[]{:S(2)}) copy-start(bf16[3,60,384]{2,1,0:T(8,128)(2,1)} %cols_ref.1) | copy-start | bytes 414724
  16.3 9.8 %copy-start.3 = (s32[384,4]{0,1:T(4,128)S(1)}, s32[384,4]{0,1:T(4,128)}, u32[]{:S(2)}) copy-start(s32[384,4]{0,1:T(4,128)} %param.17) | copy-start | bytes 18436
  16.3 9.8 %copy-start.4 = (s32[384,1]{0,1:T(1,128)S(1)}, s32[384,1]{0,1:T(1,128)}, u32[]{:S(2)}) copy-start(s32[384,1]{0,1:T(1,128)} %param.16) | copy-start | bytes 4612
  16.3 9.8 %copy-start.5 = (bf16[384,4]{0,1:T(4,128)(2,1)S(1)}, bf16[384,4]{0,1:T(4,128)(2,1)}, u32[]{:S(2)}) copy-start(bf16[384,4]{0,1:T(4,128)(2,1)} %param.18) | copy-start | bytes 9220
  26.1 52.8 %copy-start = (f32[3,8,96,128]{3,2,1,0:T(8,128)S(1)}, f32[3,8,96,128]{3,2,1,0:T(8,128)}, u32[]{:S(2)}) copy-start(f32[3,8,96,128]{3,2,1,0:T(8,128)} %param.13) | copy-start | bytes 3538948
  26.1 52.8 %copy-start.2 = (s32[96,128]{1,0:T(8,128)S(1)}, s32[96,128]{1,0:T(8,128)}, u32[]{:S(2)}) copy-start(s32[96,128]{1,0:T(8,128)} %terrain_ref.1) | copy-start | bytes 147460
  37.1 10.7 %all-to-all-start.2 = ((f32[8,24,128]{2,1,0:T(8,128)}), f32[8,24,128]{2,1,0:T(8,128)S(1)}, u32[]{:S(2)}, u32[]{:S(2)}) async-start(f32[8,24,128]{2,1,0:T(8,128)} %broadcast_in_dim.12), calls=%async_computation.2 | async-start | bytes 196608 | tf_op jit(solution)/shard_map/all_to_all | solution.py:352
  40.4 7.4 %collective-permute-start = (f32[24,128]{1,0:T(8,128)S(1)}, f32[24,128]{1,0:T(8,128)S(1)}, u32[]{:S(2)}, u32[]{:S(2)}) collective-permute-start(f32[24,128]{1,0:T(8,128)S(1)} %get-tuple-element.33), channel_id=1, source_target_pairs={{0,24},{48,72},{96,120},{144,168},{192,216},{240,264},{288,312},{3... | collective-permute-start | bytes 36872 | tf_op jit(solution)/shard_map/ppermute | solution.py:369
  43.2 4.9 %collective-permute-start.1 = (f32[24,128]{1,0:T(8,128)S(1)}, f32[24,128]{1,0:T(8,128)S(1)}, u32[]{:S(2)}, u32[]{:S(2)}) collective-permute-start(f32[24,128]{1,0:T(8,128)S(1)} %get-tuple-element.35), channel_id=1, source_target_pairs={{0,1},{2,3},{4,5},{6,7},{8,9},{10,11},{12,13},{14,15},{16,17},{18,... | collective-permute-start | bytes 36872 | tf_op jit(solution)/shard_map/ppermute | solution.py:369
  48.7 22.7 %all-to-all-start.3 = ((f32[12,24,128]{2,1,0:T(8,128)}), f32[12,24,128]{2,1,0:T(8,128)S(1)}, u32[]{:S(2)}, u32[]{:S(2)}) async-start(f32[12,24,128]{2,1,0:T(8,128)} %broadcast_in_dim.13), calls=%async_computation.3 | async-start | bytes 294912 | tf_op jit(solution)/shard_map/all_to_all | solution.py:352
  60.7 10.8 %collective-permute-start.2 = (f32[24,128]{1,0:T(8,128)S(1)}, f32[24,128]{1,0:T(8,128)S(1)}, u32[]{:S(2)}, u32[]{:S(2)}) collective-permute-start(f32[24,128]{1,0:T(8,128)S(1)} %get-tuple-element.38), channel_id=1, source_target_pairs={{24,48},{72,96},{120,144},{168,192},{216,240},{264,288},{312,336},... | collective-permute-start | bytes 36872 | tf_op jit(solution)/shard_map/ppermute | solution.py:369
  66.0 5.5 %collective-permute-start.3 = (f32[24,128]{1,0:T(8,128)S(1)}, f32[24,128]{1,0:T(8,128)S(1)}, u32[]{:S(2)}, u32[]{:S(2)}) collective-permute-start(f32[24,128]{1,0:T(8,128)S(1)} %get-tuple-element.39), channel_id=1, source_target_pairs={{1,2},{3,4},{5,6},{7,8},{9,10},{11,12},{13,14},{15,16},{17,18},{19... | collective-permute-start | bytes 36872 | tf_op jit(solution)/shard_map/ppermute | solution.py:369
  72.2 11.8 %all-to-all-start.4 = ((f32[8,24,128]{2,1,0:T(8,128)}), f32[8,24,128]{2,1,0:T(8,128)S(1)}, u32[]{:S(2)}, u32[]{:S(2)}) async-start(f32[8,24,128]{2,1,0:T(8,128)} %broadcast_in_dim.14), calls=%async_computation.4 | async-start | bytes 196608 | tf_op jit(solution)/shard_map/all_to_all | solution.py:352

commit v5 on v4

--- a/solution.py
+++ b/solution.py
@@ -452,12 +452,14 @@
         axis=0,
     )
     mine, xa, xb, ya, yb = lax.optimization_barrier((mine, xa, xb, ya, yb))
-    ya, xa = swap(ya, "gy", 0), swap(xa, "gx", 0)
+    xb = swap(xb, "gx", 1)
     mine = jnp.sum(gather(mine, ("gx", "gy"), tall_groups), axis=0)
     mine, xa, xb, ya, yb = lax.optimization_barrier((mine, xa, xb, ya, yb))
-    xb, yb = swap(xb, "gx", 1), swap(yb, "gy", 1)
+    yb, ya = swap(yb, "gy", 1), swap(ya, "gy", 0)
     mine = jnp.sum(gather(mine, "gy", deep_groups), axis=0)
-    mine, xb, yb = lax.optimization_barrier((mine, xb, yb))
+    mine, ya, yb = lax.optimization_barrier((mine, ya, yb))
+    mine, xa = lax.optimization_barrier((mine, xa))
+    xa = swap(xa, "gx", 0)
     nudge = gather(mine, "gx", wide_groups).reshape(part.shape)
 
     state, low_x, low_y = call(

time: 86.1 us -> 85.9 us (level)
  starting transfers between devices: 48.4 us -> 46.5 us
  waiting for transfers between devices: 16.9 us -> 18.5 us
    ppermute x4, starting transfers between devices: 12.2 us -> 10.4 us  [swap(): return lax.ppermute(piece, axis, pairs + [(j, i) for i, j in pairs])]
where the time goes in v5:
time: 85.9 us; the launch traced here: 85.3 us
  starting transfers between devices  46.5 us (54%)
  waiting for transfers between devices  18.5 us (22%)
  Pallas kernels  8 us (9%)
  blocking collectives  7.75 us (9%)
  local copies, waits for them, and re-layouts  3.62 us (4%)
    all_to_all x4, starting transfers between devices, gather(): lax.all_to_all(jnp.broadcast_to(piece[None], (count,) + piece.shape), axi...  36.1 us
    all_to_all x4, waiting for transfers between devices, gather(): lax.all_to_all(jnp.broadcast_to(piece[None], (count,) + piece.shape), axi...  17.4 us
    ppermute x4, starting transfers between devices, swap(): return lax.ppermute(piece, axis, pairs + [(j, i) for i, j in pairs])  10.4 us
    pallas_call x4, Pallas kernels, call(): pl.pallas_call(kernel, out_shape=[jax.ShapeDtypeStruct(s, d) for s, d in...  8 us
    all_to_all x1, blocking collectives, per_device(): lax.all_to_all(pieces, 'gx', 0, 0, axis_index_groups=wide_groups, tiled=T...  7.75 us
    broadcast_in_dim x5, local copies, waits for them, and re-layouts, gather(): jnp.broadcast_to(piece[None], (count,) + piece.shape)  2.61 us
  transfers between devices with their start and end apart: 8, of which 5 were waited for; matrix products, arithmetic and copies ran while one was open for 0% of the time, Pallas kernels for 5%

profile of v5, /device:TPU:1, one launch (start us, length us, event | category | flops | bytes accessed | tf_op | source)
XLA Modules:
  0.0 85.3 jit_solution(1421395213279969795)
XLA Ops:
  0.6 0.9 %slice.3 = s32[12,16]{1,0:T(8,128)S(1)} slice(s32[96,128]{1,0:T(8,128)} %terrain_ref.1), slice={[0:96:8], [0:128:8]} | slice | bytes 1536 | tf_op jit(solution)/shard_map/slice | solution.py:406
  1.5 0.1 reshape.23
  1.6 0.6 broadcast_in_dim.11
  2.3 14.0 %all-to-all-start = ((f32[32,2,128]{2,1,0:T(2,128)}), f32[32,2,128]{2,1,0:T(2,128)S(1)}, u32[]{:S(2)}, u32[]{:S(2)}) async-start(f32[32,2,128]{2,1,0:T(2,128)} %broadcast_in_dim.11), calls=%async_computation | async-start | bytes 65536 | tf_op jit(solution)/shard_map/all_to_all | solution.py:352
  16.3 2.3 %shard_map.140 = (f32[32,768]{1,0:T(8,128)S(1)}, bf16[64,1536]{1,0:T(8,128)(2,1)S(1)}, f32[24,128]{1,0:T(8,128)S(1)}, f32[24,128]{1,0:T(8,128)S(1)}, f32[24,128]{1,0:T(8,128)S(1)}, /*index=5*/f32[24,128]{1,0:T(8,128)S(1)}) custom-call(f32[24,96,128]{2,1,0:T(8,128)} %bitcast.12, bf16[32,64,96]{2,1,0:T(8,128)(2,1)} %constant.18.clone.bx_hbm, ...), custom_call_target="tpu_custom_call" | custom-call | tf_op jit(solution)/shard_map/pallas_call | solution.py:335
  18.7 7.4 %all-to-all-done = f32[32,2,128]{2,1,0:T(2,128)S(1)} async-done(((f32[32,2,128]{2,1,0:T(2,128)}), f32[32,2,128]{2,1,0:T(2,128)S(1)}, u32[]{:S(2)}, u32[]{:S(2)}) %all-to-all-start) | async-done | bytes 32800 | tf_op jit(solution)/shard_map/all_to_all | solution.py:352
  26.1 2.5 %shard_map.141 = f32[8,24,128]{2,1,0:T(8,128)S(1)} custom-call(f32[32,256]{1,0:T(8,128)S(1)} %bitcast.14, s32[1,384]{1,0:T(1,128)S(1)} %bitcast.18, s32[4,384]{1,0:T(4,128)S(1)} %bitcast.16, bf16[4,384]{1,0:T(4,128)(2,1)S(1)} %bitcast.19, bf16[3,60,384]{2,1,0:T(8,128)(2,1)S(1)} %copy-done.1, bf16[64,1536]{1,0:T(8,128)(2,1)S(1)} %get-tuple-element.28.look_ref, ...), custom_call_target="tpu_custom_call" | custom-call | tf_op jit(solution)/shard_map/pallas_call | solution.py:335
  28.6 7.8 %all_to_all.25 = f32[8,24,128]{2,1,0:T(8,128)S(1)} all-to-all(f32[8,24,128]{2,1,0:T(8,128)S(1)} %shard_map.141), channel_id=1, replica_groups={{0,24,192,216,384,408,576,600},{48,72,240,264,432,456,624,648},{96,120,..., dimensions={0} | all-to-all | bytes 196608 | tf_op jit(solution)/shard_map/all_to_all | solution.py:449
  36.4 0.6 broadcast_in_dim.12
  37.1 3.4 %all-to-all-start.2 = ((f32[8,24,128]{2,1,0:T(8,128)}), f32[8,24,128]{2,1,0:T(8,128)S(1)}, u32[]{:S(2)}, u32[]{:S(2)}) async-start(f32[8,24,128]{2,1,0:T(8,128)} %broadcast_in_dim.12), calls=%async_computation.2 | async-start | bytes 196608 | tf_op jit(solution)/shard_map/all_to_all | solution.py:352
  40.4 5.1 %collective-permute-start = (f32[24,128]{1,0:T(8,128)S(1)}, f32[24,128]{1,0:T(8,128)S(1)}, u32[]{:S(2)}, u32[]{:S(2)}) collective-permute-start(f32[24,128]{1,0:T(8,128)S(1)} %get-tuple-element.36), channel_id=1, source_target_pairs={{24,48},{72,96},{120,144},{168,192},{216,240},{264,288},{312,336},... | collective-permute-start | bytes 36872 | tf_op jit(solution)/shard_map/ppermute | solution.py:369
  45.6 2.2 %all-to-all-done.2 = f32[8,24,128]{2,1,0:T(8,128)S(1)} async-done(((f32[8,24,128]{2,1,0:T(8,128)}), f32[8,24,128]{2,1,0:T(8,128)S(1)}, u32[]{:S(2)}, u32[]{:S(2)}) %all-to-all-start.2) | async-done | bytes 98336 | tf_op jit(solution)/shard_map/all_to_all | solution.py:352
  47.8 0.7 broadcast_in_dim.13
  48.5 12.0 %all-to-all-start.3 = ((f32[12,24,128]{2,1,0:T(8,128)}), f32[12,24,128]{2,1,0:T(8,128)S(1)}, u32[]{:S(2)}, u32[]{:S(2)}) async-start(f32[12,24,128]{2,1,0:T(8,128)} %broadcast_in_dim.13), calls=%async_computation.3 | async-start | bytes 294912 | tf_op jit(solution)/shard_map/all_to_all | solution.py:352
  60.5 2.6 %collective-permute-start.1 = (f32[24,128]{1,0:T(8,128)S(1)}, f32[24,128]{1,0:T(8,128)S(1)}, u32[]{:S(2)}, u32[]{:S(2)}) collective-permute-start(f32[24,128]{1,0:T(8,128)S(1)} %get-tuple-element.40), channel_id=1, source_target_pairs={{0,1},{2,3},{4,5},{6,7},{8,9},{10,11},{12,13},{14,15},{16,17},{18,... | collective-permute-start | bytes 36872 | tf_op jit(solution)/shard_map/ppermute | solution.py:369
  63.0 0.7 collective-permute-start.2
  63.7 7.5 %all-to-all-done.3 = f32[12,24,128]{2,1,0:T(8,128)S(1)} async-done(((f32[12,24,128]{2,1,0:T(8,128)}), f32[12,24,128]{2,1,0:T(8,128)S(1)}, u32[]{:S(2)}, u32[]{:S(2)}) %all-to-all-start.3) | async-done | bytes 147488 | tf_op jit(solution)/shard_map/all_to_all | solution.py:352
  71.3 0.6 broadcast_in_dim.14
  71.9 6.8 %all-to-all-start.4 = ((f32[8,24,128]{2,1,0:T(8,128)}), f32[8,24,128]{2,1,0:T(8,128)S(1)}, u32[]{:S(2)}, u32[]{:S(2)}) async-start(f32[8,24,128]{2,1,0:T(8,128)} %broadcast_in_dim.14), calls=%async_computation.4 | async-start | bytes 196608 | tf_op jit(solution)/shard_map/all_to_all | solution.py:352
  78.7 2.0 %collective-permute-start.3 = (f32[24,128]{1,0:T(8,128)S(1)}, f32[24,128]{1,0:T(8,128)S(1)}, u32[]{:S(2)}, u32[]{:S(2)}) collective-permute-start(f32[24,128]{1,0:T(8,128)S(1)} %get-tuple-element.45), channel_id=1, source_target_pairs={{0,24},{48,72},{96,120},{144,168},{192,216},{240,264},{288,312},{3... | collective-permute-start | bytes 36872 | tf_op jit(solution)/shard_map/ppermute | solution.py:369
  80.7 1.0 %collective-permute-done.3.xa_ref = f32[24,128]{1,0:T(8,128)S(1)} collective-permute-done((f32[24,128]{1,0:T(8,128)S(1)}, f32[24,128]{1,0:T(8,128)S(1)}, u32[]{:S(2)}, u32[]{:S(2)}) %collective-permute-start.3) | collective-permute-done | bytes 12320 | tf_op jit(solution)/shard_map/ppermute | solution.py:369
  81.8 1.6 %shard_map.142 = (f32[24,96,128]{2,1,0:T(8,128)S(1)}, bf16[96,96]{1,0:T(8,128)(2,1)S(1)}, bf16[384,512]{1,0:T(8,128)(2,1)S(1)}) custom-call(f32[24,128]{1,0:T(8,128)S(1)} %reduce_sum.29.after, f32[24,96,128]{2,1,0:T(8,128)S(1)} %bitcast.13, s32[96,128]{1,0:T(8,128)S(1)} %copy-done.2, f32[24,128]{1,0:T(8,128)S(1)} %collective-permute-done.3.xa_ref, ...), custom_call_target="tpu_custom_call" | custom-call | tf_op jit(solution)/shard_map/pallas_call | solution.py:335
  83.4 0.3 all-to-all-done.4.n_ref
  83.7 1.6 %shard_map.143 = (f32[24,96,128]{2,1,0:T(8,128)}, f32[24,32,32]{2,1,0:T(8,128)}) custom-call(f32[24,96,128]{2,1,0:T(8,128)S(1)} %get-tuple-element.49.state_ref, f32[8,24,128]{2,1,0:T(8,128)S(1)} %all-to-all-done.4.n_ref, bf16[96,96]{1,0:T(8,128)(2,1)S(1)} %get-tuple-element.50.bx_ref, bf16[384,512]{1,0:T(8,128)(2,1)S(1)} %get-tuple-element.51.right_ref), custom_call_target="tpu_custom_call" | custom-call | tf_op jit(solution)/shard_map/pallas_call | solution.py:335
  (21 shorter events, 0.1 us)
Async XLA Ops:
  2.3 23.8 %all-to-all-start = ((f32[32,2,128]{2,1,0:T(2,128)}), f32[32,2,128]{2,1,0:T(2,128)S(1)}, u32[]{:S(2)}, u32[]{:S(2)}) async-start(f32[32,2,128]{2,1,0:T(2,128)} %broadcast_in_dim.11), calls=%async_computation | async-start | bytes 65536 | tf_op jit(solution)/shard_map/all_to_all | solution.py:352
  16.3 9.8 %copy-start.1 = (bf16[3,60,384]{2,1,0:T(8,128)(2,1)S(1)}, bf16[3,60,384]{2,1,0:T(8,128)(2,1)}, u32[]{:S(2)}) copy-start(bf16[3,60,384]{2,1,0:T(8,128)(2,1)} %cols_ref.1) | copy-start | bytes 414724
  16.3 9.8 %copy-start.3 = (s32[384,4]{0,1:T(4,128)S(1)}, s32[384,4]{0,1:T(4,128)}, u32[]{:S(2)}) copy-start(s32[384,4]{0,1:T(4,128)} %param.17) | copy-start | bytes 18436
  16.3 9.8 %copy-start.4 = (s32[384,1]{0,1:T(1,128)S(1)}, s32[384,1]{0,1:T(1,128)}, u32[]{:S(2)}) copy-start(s32[384,1]{0,1:T(1,128)} %param.16) | copy-start | bytes 4612
  16.3 9.8 %copy-start.5 = (bf16[384,4]{0,1:T(4,128)(2,1)S(1)}, bf16[384,4]{0,1:T(4,128)(2,1)}, u32[]{:S(2)}) copy-start(bf16[384,4]{0,1:T(4,128)(2,1)} %param.18) | copy-start | bytes 9220
  26.1 55.7 %copy-start = (f32[3,8,96,128]{3,2,1,0:T(8,128)S(1)}, f32[3,8,96,128]{3,2,1,0:T(8,128)}, u32[]{:S(2)}) copy-start(f32[3,8,96,128]{3,2,1,0:T(8,128)} %param.13) | copy-start | bytes 3538948
  26.1 55.7 %copy-start.2 = (s32[96,128]{1,0:T(8,128)S(1)}, s32[96,128]{1,0:T(8,128)}, u32[]{:S(2)}) copy-start(s32[96,128]{1,0:T(8,128)} %terrain_ref.1) | copy-start | bytes 147460
  37.1 10.7 %all-to-all-start.2 = ((f32[8,24,128]{2,1,0:T(8,128)}), f32[8,24,128]{2,1,0:T(8,128)S(1)}, u32[]{:S(2)}, u32[]{:S(2)}) async-start(f32[8,24,128]{2,1,0:T(8,128)} %broadcast_in_dim.12), calls=%async_computation.2 | async-start | bytes 196608 | tf_op jit(solution)/shard_map/all_to_all | solution.py:352
  40.4 7.4 %collective-permute-start = (f32[24,128]{1,0:T(8,128)S(1)}, f32[24,128]{1,0:T(8,128)S(1)}, u32[]{:S(2)}, u32[]{:S(2)}) collective-permute-start(f32[24,128]{1,0:T(8,128)S(1)} %get-tuple-element.36), channel_id=1, source_target_pairs={{24,48},{72,96},{120,144},{168,192},{216,240},{264,288},{312,336},... | collective-permute-start | bytes 36872 | tf_op jit(solution)/shard_map/ppermute | solution.py:369
  48.5 22.7 %all-to-all-start.3 = ((f32[12,24,128]{2,1,0:T(8,128)}), f32[12,24,128]{2,1,0:T(8,128)S(1)}, u32[]{:S(2)}, u32[]{:S(2)}) async-start(f32[12,24,128]{2,1,0:T(8,128)} %broadcast_in_dim.13), calls=%async_computation.3 | async-start | bytes 294912 | tf_op jit(solution)/shard_map/all_to_all | solution.py:352
  60.5 10.8 %collective-permute-start.1 = (f32[24,128]{1,0:T(8,128)S(1)}, f32[24,128]{1,0:T(8,128)S(1)}, u32[]{:S(2)}, u32[]{:S(2)}) collective-permute-start(f32[24,128]{1,0:T(8,128)S(1)} %get-tuple-element.40), channel_id=1, source_target_pairs={{0,1},{2,3},{4,5},{6,7},{8,9},{10,11},{12,13},{14,15},{16,17},{18,... | collective-permute-start | bytes 36872 | tf_op jit(solution)/shard_map/ppermute | solution.py:369
  63.0 8.2 %collective-permute-start.2 = (f32[24,128]{1,0:T(8,128)S(1)}, f32[24,128]{1,0:T(8,128)S(1)}, u32[]{:S(2)}, u32[]{:S(2)}) collective-permute-start(f32[24,128]{1,0:T(8,128)S(1)} %get-tuple-element.41), channel_id=1, source_target_pairs={{1,2},{3,4},{5,6},{7,8},{9,10},{11,12},{13,14},{15,16},{17,18},{19... | collective-permute-start | bytes 36872 | tf_op jit(solution)/shard_map/ppermute | solution.py:369
  71.9 11.8 %all-to-all-start.4 = ((f32[8,24,128]{2,1,0:T(8,128)}), f32[8,24,128]{2,1,0:T(8,128)S(1)}, u32[]{:S(2)}, u32[]{:S(2)}) async-start(f32[8,24,128]{2,1,0:T(8,128)} %broadcast_in_dim.14), calls=%async_computation.4 | async-start | bytes 196608 | tf_op jit(solution)/shard_map/all_to_all | solution.py:352
  78.7 3.1 %collective-permute-start.3 = (f32[24,128]{1,0:T(8,128)S(1)}, f32[24,128]{1,0:T(8,128)S(1)}, u32[]{:S(2)}, u32[]{:S(2)}) collective-permute-start(f32[24,128]{1,0:T(8,128)S(1)} %get-tuple-element.45), channel_id=1, source_target_pairs={{0,24},{48,72},{96,120},{144,168},{192,216},{240,264},{288,312},{3... | collective-permute-start | bytes 36872 | tf_op jit(solution)/shard_map/ppermute | solution.py:369

commit v6 on v5

--- a/solution.py
+++ b/solution.py
@@ -236,7 +236,7 @@
 
 
 def stencil_kernel(
-    after, f_ref, terrain_ref, xa_ref, xb_ref, ya_ref, yb_ref, bx_hbm, by_hbm, out_ref, bx_ref, right_ref,
+    after, f_ref, terrain_ref, xb_ref, ya_ref, yb_ref, bx_hbm, by_hbm, out_ref, bx_ref, right_ref, gain_ref,
     east_ref, west_ref, by_ref, bx_sem, by_sem, *, variables
 ):
     bx_copy = pltpu.make_async_copy(bx_hbm.at[lax.axis_index("gx")], bx_ref, bx_sem)
@@ -246,7 +246,13 @@
     count, cells_x, cells_y = f_ref.shape
     levels = count // variables
     row, lane = rows_lanes((cells_x, cells_y))
-    east_ref[...], west_ref[...] = by_parity("gx", xa_ref[...], xb_ref[...])
+    other = xb_ref[...]
+    east_ref[...], west_ref[...] = by_parity("gx", jnp.zeros_like(other), other)
+    first = lax.rem(lax.axis_index("gx"), 2) == 0
+    for k in range(levels):
+        gain_ref[k : k + 1, :] = 0.1 + 0.05 * jnp.where(
+            first, -f_ref[k, cells_x - 1 : cells_x, :], f_ref[k, 0:1, :]
+        )
     north, south = by_parity("gy", ya_ref[...], yb_ref[...])
     south = jnp.transpose(south)
     north = jnp.transpose(north)
@@ -280,11 +286,13 @@
 
 
 def nudge_kernel(
-    state_ref, n_ref, bx_ref, right_ref, out_hbm, coeffs_hbm, out_ref, coeffs_ref, low_ref, out_sem, coeffs_sem
+    state_ref, n_ref, bx_ref, right_ref, gain_ref, xa_ref, out_hbm, coeffs_hbm, out_ref, coeffs_ref, low_ref, out_sem, coeffs_sem
 ):
     count, cells_x, cells_y = state_ref.shape
     per = LANES // KW
     groups = count // per
+    levels = gain_ref.shape[0]
+    edge = lax.rem(lax.axis_index("gx") + 1, 2) * (cells_x - 1)
     nudge = jnp.concatenate(
         [
             jnp.concatenate([n_ref[:, m * groups + g, :] for m in range(KW // 8)], axis=0)
@@ -316,6 +324,8 @@
                 out_ref[i] = state_ref[i] + low_ref[
                     g * cells_x : (g + 1) * cells_x, q * cells_y : (q + 1) * cells_y
                 ]
+                k = i % levels
+                out_ref[i, pl.ds(edge, 1), :] += xa_ref[i : i + 1, :] * gain_ref[k : k + 1, :]
             at = pl.ds(per * (third * some + g), per)
             copies.append(
                 pltpu.make_async_copy(out_ref.at[at], out_hbm.at[at], out_sem.at[third * some + g])
@@ -462,22 +472,23 @@
     xa = swap(xa, "gx", 0)
     nudge = gather(mine, "gx", wide_groups).reshape(part.shape)
 
-    state, low_x, low_y = call(
+    state, low_x, low_y, gain = call(
         functools.partial(stencil_kernel, variables=variables),
-        (mine, f, terrain, xa, xb, ya, yb, tab_low_x, tab_low_y),
-        [LOOSE] + [NEAR] * 6 + [FAR] * 2,
+        (mine, f, terrain, xb, ya, yb, tab_low_x, tab_low_y),
+        [LOOSE] + [NEAR] * 5 + [FAR] * 2,
         [
             (f.shape, f32),
             (tab_low_x.shape[1:], b16),
             (tab_low_y.shape[1:2] + (per * cells_y,), b16),
-        ],
-        [NEAR] * 3,
-        [pltpu.VMEM(xa.shape, f32)] * 2 + [pltpu.VMEM(tab_low_y.shape[1:], b16), DMA, DMA],
+            ((levels, cells_y), f32),
+        ],
+        [NEAR] * 4,
+        [pltpu.VMEM(xb.shape, f32)] * 2 + [pltpu.VMEM(tab_low_y.shape[1:], b16), DMA, DMA],
     )
     updated, coeffs = call(
         nudge_kernel,
-        (state, nudge, low_x, low_y),
-        [NEAR] * 4,
+        (state, nudge, low_x, low_y, gain, xa),
+        [NEAR] * 6,
         [(f.shape, f32), ((count, KW, KW), f32)],
         [FAR, FAR],
         [

time: 85.9 us -> 85.9 us (level)
    ppermute x4, waiting for transfers between devices: 1.05 us -> 0.01 us  [swap(): return lax.ppermute(piece, axis, pairs + [(j, i) for i, j in pairs])]
  transfers between devices with their start and end apart: 8 -> 8, of which waited for: 5 -> 4; matrix products, arithmetic and copies ran while one was open for 0% -> 0% of each run, Pallas kernels for 5% -> 5%
where the time goes in v6:
time: 85.9 us; the launch traced here: 85.3 us
  starting transfers between devices  46.5 us (54%)
  waiting for transfers between devices  17.9 us (21%)
  Pallas kernels  8.56 us (10%)
  blocking collectives  7.75 us (9%)
  local copies, waits for them, and re-layouts  3.62 us (4%)
    all_to_all x4, starting transfers between devices, gather(): lax.all_to_all(jnp.broadcast_to(piece[None], (count,) + piece.shape), axi...  36.1 us
    all_to_all x4, waiting for transfers between devices, gather(): lax.all_to_all(jnp.broadcast_to(piece[None], (count,) + piece.shape), axi...  17.9 us
    ppermute x4, starting transfers between devices, swap(): return lax.ppermute(piece, axis, pairs + [(j, i) for i, j in pairs])  10.4 us
    pallas_call x4, Pallas kernels, call(): pl.pallas_call(kernel, out_shape=[jax.ShapeDtypeStruct(s, d) for s, d in...  8.56 us
    all_to_all x1, blocking collectives, per_device(): lax.all_to_all(pieces, 'gx', 0, 0, axis_index_groups=wide_groups, tiled=T...  7.75 us
    broadcast_in_dim x5, local copies, waits for them, and re-layouts, gather(): jnp.broadcast_to(piece[None], (count,) + piece.shape)  2.61 us
  transfers between devices with their start and end apart: 8, of which 4 were waited for; matrix products, arithmetic and copies ran while one was open for 0% of the time, Pallas kernels for 5%

profile of v6, /device:TPU:1, one launch (start us, length us, event | category | flops | bytes accessed | tf_op | source)
XLA Modules:
  0.0 85.3 jit_solution(15699626446282791641)
XLA Ops:
  0.6 0.9 %slice.3 = s32[12,16]{1,0:T(8,128)S(1)} slice(s32[96,128]{1,0:T(8,128)} %terrain_ref.1), slice={[0:96:8], [0:128:8]} | slice | bytes 1536 | tf_op jit(solution)/shard_map/slice | solution.py:416
  1.5 0.1 reshape.23
  1.6 0.6 broadcast_in_dim.11
  2.3 14.0 %all-to-all-start = ((f32[32,2,128]{2,1,0:T(2,128)}), f32[32,2,128]{2,1,0:T(2,128)S(1)}, u32[]{:S(2)}, u32[]{:S(2)}) async-start(f32[32,2,128]{2,1,0:T(2,128)} %broadcast_in_dim.11), calls=%async_computation | async-start | bytes 65536 | tf_op jit(solution)/shard_map/all_to_all | solution.py:362
  16.3 0.0 copy-start.3
  16.3 2.3 %shard_map.140 = (f32[32,768]{1,0:T(8,128)S(1)}, bf16[64,1536]{1,0:T(8,128)(2,1)S(1)}, f32[24,128]{1,0:T(8,128)S(1)}, f32[24,128]{1,0:T(8,128)S(1)}, f32[24,128]{1,0:T(8,128)S(1)}, /*index=5*/f32[24,128]{1,0:T(8,128)S(1)}) custom-call(f32[24,96,128]{2,1,0:T(8,128)} %bitcast.12, bf16[32,64,96]{2,1,0:T(8,128)(2,1)} %constant.18.clone.bx_hbm, ...), custom_call_target="tpu_custom_call" | custom-call | tf_op jit(solution)/shard_map/pallas_call | solution.py:345
  18.7 7.4 %all-to-all-done = f32[32,2,128]{2,1,0:T(2,128)S(1)} async-done(((f32[32,2,128]{2,1,0:T(2,128)}), f32[32,2,128]{2,1,0:T(2,128)S(1)}, u32[]{:S(2)}, u32[]{:S(2)}) %all-to-all-start) | async-done | bytes 32800 | tf_op jit(solution)/shard_map/all_to_all | solution.py:362
  26.1 2.5 %shard_map.141 = f32[8,24,128]{2,1,0:T(8,128)S(1)} custom-call(f32[32,256]{1,0:T(8,128)S(1)} %bitcast.14, s32[1,384]{1,0:T(1,128)S(1)} %bitcast.18, s32[4,384]{1,0:T(4,128)S(1)} %bitcast.16, bf16[4,384]{1,0:T(4,128)(2,1)S(1)} %bitcast.19, bf16[3,60,384]{2,1,0:T(8,128)(2,1)S(1)} %copy-done.1, bf16[64,1536]{1,0:T(8,128)(2,1)S(1)} %get-tuple-element.29.look_ref, ...), custom_call_target="tpu_custom_call" | custom-call | tf_op jit(solution)/shard_map/pallas_call | solution.py:345
  28.6 7.8 %all_to_all.25 = f32[8,24,128]{2,1,0:T(8,128)S(1)} all-to-all(f32[8,24,128]{2,1,0:T(8,128)S(1)} %shard_map.141), channel_id=1, replica_groups={{0,24,192,216,384,408,576,600},{48,72,240,264,432,456,624,648},{96,120,..., dimensions={0} | all-to-all | bytes 196608 | tf_op jit(solution)/shard_map/all_to_all | solution.py:459
  36.4 0.6 broadcast_in_dim.12
  37.1 3.4 %all-to-all-start.2 = ((f32[8,24,128]{2,1,0:T(8,128)}), f32[8,24,128]{2,1,0:T(8,128)S(1)}, u32[]{:S(2)}, u32[]{:S(2)}) async-start(f32[8,24,128]{2,1,0:T(8,128)} %broadcast_in_dim.12), calls=%async_computation.2 | async-start | bytes 196608 | tf_op jit(solution)/shard_map/all_to_all | solution.py:362
  40.4 5.1 %collective-permute-start = (f32[24,128]{1,0:T(8,128)S(1)}, f32[24,128]{1,0:T(8,128)S(1)}, u32[]{:S(2)}, u32[]{:S(2)}) collective-permute-start(f32[24,128]{1,0:T(8,128)S(1)} %get-tuple-element.37), channel_id=1, source_target_pairs={{24,48},{72,96},{120,144},{168,192},{216,240},{264,288},{312,336},... | collective-permute-start | bytes 36872 | tf_op jit(solution)/shard_map/ppermute | solution.py:379
  45.6 2.2 %all-to-all-done.2 = f32[8,24,128]{2,1,0:T(8,128)S(1)} async-done(((f32[8,24,128]{2,1,0:T(8,128)}), f32[8,24,128]{2,1,0:T(8,128)S(1)}, u32[]{:S(2)}, u32[]{:S(2)}) %all-to-all-start.2) | async-done | bytes 98336 | tf_op jit(solution)/shard_map/all_to_all | solution.py:362
  47.8 0.7 broadcast_in_dim.13
  48.5 12.0 %all-to-all-start.3 = ((f32[12,24,128]{2,1,0:T(8,128)}), f32[12,24,128]{2,1,0:T(8,128)S(1)}, u32[]{:S(2)}, u32[]{:S(2)}) async-start(f32[12,24,128]{2,1,0:T(8,128)} %broadcast_in_dim.13), calls=%async_computation.3 | async-start | bytes 294912 | tf_op jit(solution)/shard_map/all_to_all | solution.py:362
  60.5 2.6 %collective-permute-start.1 = (f32[24,128]{1,0:T(8,128)S(1)}, f32[24,128]{1,0:T(8,128)S(1)}, u32[]{:S(2)}, u32[]{:S(2)}) collective-permute-start(f32[24,128]{1,0:T(8,128)S(1)} %get-tuple-element.41), channel_id=1, source_target_pairs={{0,1},{2,3},{4,5},{6,7},{8,9},{10,11},{12,13},{14,15},{16,17},{18,... | collective-permute-start | bytes 36872 | tf_op jit(solution)/shard_map/ppermute | solution.py:379
  63.0 0.7 collective-permute-start.2
  63.7 7.5 %all-to-all-done.3 = f32[12,24,128]{2,1,0:T(8,128)S(1)} async-done(((f32[12,24,128]{2,1,0:T(8,128)}), f32[12,24,128]{2,1,0:T(8,128)S(1)}, u32[]{:S(2)}, u32[]{:S(2)}) %all-to-all-start.3) | async-done | bytes 147488 | tf_op jit(solution)/shard_map/all_to_all | solution.py:362
  71.3 0.6 broadcast_in_dim.14
  71.9 6.8 %all-to-all-start.4 = ((f32[8,24,128]{2,1,0:T(8,128)}), f32[8,24,128]{2,1,0:T(8,128)S(1)}, u32[]{:S(2)}, u32[]{:S(2)}) async-start(f32[8,24,128]{2,1,0:T(8,128)} %broadcast_in_dim.14), calls=%async_computation.4 | async-start | bytes 196608 | tf_op jit(solution)/shard_map/all_to_all | solution.py:362
  78.7 2.0 %collective-permute-start.3 = (f32[24,128]{1,0:T(8,128)S(1)}, f32[24,128]{1,0:T(8,128)S(1)}, u32[]{:S(2)}, u32[]{:S(2)}) collective-permute-start(f32[24,128]{1,0:T(8,128)S(1)} %get-tuple-element.53), channel_id=1, source_target_pairs={{0,24},{48,72},{96,120},{144,168},{192,216},{240,264},{288,312},{3... | collective-permute-start | bytes 36872 | tf_op jit(solution)/shard_map/ppermute | solution.py:379
  80.7 2.2 %shard_map.142 = (f32[24,96,128]{2,1,0:T(8,128)S(1)}, bf16[96,96]{1,0:T(8,128)(2,1)S(1)}, bf16[384,512]{1,0:T(8,128)(2,1)S(1)}, f32[8,128]{1,0:T(8,128)S(1)}) custom-call(f32[24,128]{1,0:T(8,128)S(1)} %reduce_sum.29.after, f32[24,96,128]{2,1,0:T(8,128)S(1)} %bitcast.13, s32[96,128]{1,0:T(8,128)S(1)} %copy-done.2, f32[24,128]{1,0:T(8,128)S(1)} %collective-permute-done.xb_ref, ...), custom_call_target="tpu_custom_call" | custom-call | tf_op jit(solution)/shard_map/pallas_call | solution.py:345
  82.9 0.8 all-to-all-done.4.n_ref
  83.7 1.6 %shard_map.143 = (f32[24,96,128]{2,1,0:T(8,128)}, f32[24,32,32]{2,1,0:T(8,128)}) custom-call(f32[24,96,128]{2,1,0:T(8,128)S(1)} %get-tuple-element.49.state_ref, f32[8,24,128]{2,1,0:T(8,128)S(1)} %all-to-all-done.4.n_ref, bf16[96,96]{1,0:T(8,128)(2,1)S(1)} %get-tuple-element.50.bx_ref, bf16[384,512]{1,0:T(8,128)(2,1)S(1)} %get-tuple-element.51.right_ref, ...), custom_call_target="tpu_custom_call" | custom-call | tf_op jit(solution)/shard_map/pallas_call | solution.py:345
  (21 shorter events, 0.1 us)
Async XLA Ops:
  2.3 23.8 %all-to-all-start = ((f32[32,2,128]{2,1,0:T(2,128)}), f32[32,2,128]{2,1,0:T(2,128)S(1)}, u32[]{:S(2)}, u32[]{:S(2)}) async-start(f32[32,2,128]{2,1,0:T(2,128)} %broadcast_in_dim.11), calls=%async_computation | async-start | bytes 65536 | tf_op jit(solution)/shard_map/all_to_all | solution.py:362
  16.3 9.8 %copy-start.1 = (bf16[3,60,384]{2,1,0:T(8,128)(2,1)S(1)}, bf16[3,60,384]{2,1,0:T(8,128)(2,1)}, u32[]{:S(2)}) copy-start(bf16[3,60,384]{2,1,0:T(8,128)(2,1)} %cols_ref.1) | copy-start | bytes 414724
  16.3 9.8 %copy-start.3 = (s32[384,4]{0,1:T(4,128)S(1)}, s32[384,4]{0,1:T(4,128)}, u32[]{:S(2)}) copy-start(s32[384,4]{0,1:T(4,128)} %param.17) | copy-start | bytes 18436
  16.3 9.8 %copy-start.4 = (s32[384,1]{0,1:T(1,128)S(1)}, s32[384,1]{0,1:T(1,128)}, u32[]{:S(2)}) copy-start(s32[384,1]{0,1:T(1,128)} %param.16) | copy-start | bytes 4612
  16.3 9.8 %copy-start.5 = (bf16[384,4]{0,1:T(4,128)(2,1)S(1)}, bf16[384,4]{0,1:T(4,128)(2,1)}, u32[]{:S(2)}) copy-start(bf16[384,4]{0,1:T(4,128)(2,1)} %param.18) | copy-start | bytes 9220
  26.1 54.6 %copy-start = (f32[3,8,96,128]{3,2,1,0:T(8,128)S(1)}, f32[3,8,96,128]{3,2,1,0:T(8,128)}, u32[]{:S(2)}) copy-start(f32[3,8,96,128]{3,2,1,0:T(8,128)} %param.13) | copy-start | bytes 3538948
  26.1 54.6 %copy-start.2 = (s32[96,128]{1,0:T(8,128)S(1)}, s32[96,128]{1,0:T(8,128)}, u32[]{:S(2)}) copy-start(s32[96,128]{1,0:T(8,128)} %terrain_ref.1) | copy-start | bytes 147460
  37.1 10.7 %all-to-all-start.2 = ((f32[8,24,128]{2,1,0:T(8,128)}), f32[8,24,128]{2,1,0:T(8,128)S(1)}, u32[]{:S(2)}, u32[]{:S(2)}) async-start(f32[8,24,128]{2,1,0:T(8,128)} %broadcast_in_dim.12), calls=%async_computation.2 | async-start | bytes 196608 | tf_op jit(solution)/shard_map/all_to_all | solution.py:362
  40.4 7.4 %collective-permute-start = (f32[24,128]{1,0:T(8,128)S(1)}, f32[24,128]{1,0:T(8,128)S(1)}, u32[]{:S(2)}, u32[]{:S(2)}) collective-permute-start(f32[24,128]{1,0:T(8,128)S(1)} %get-tuple-element.37), channel_id=1, source_target_pairs={{24,48},{72,96},{120,144},{168,192},{216,240},{264,288},{312,336},... | collective-permute-start | bytes 36872 | tf_op jit(solution)/shard_map/ppermute | solution.py:379
  48.5 22.7 %all-to-all-start.3 = ((f32[12,24,128]{2,1,0:T(8,128)}), f32[12,24,128]{2,1,0:T(8,128)S(1)}, u32[]{:S(2)}, u32[]{:S(2)}) async-start(f32[12,24,128]{2,1,0:T(8,128)} %broadcast_in_dim.13), calls=%async_computation.3 | async-start | bytes 294912 | tf_op jit(solution)/shard_map/all_to_all | solution.py:362
  60.5 10.8 %collective-permute-start.1 = (f32[24,128]{1,0:T(8,128)S(1)}, f32[24,128]{1,0:T(8,128)S(1)}, u32[]{:S(2)}, u32[]{:S(2)}) collective-permute-start(f32[24,128]{1,0:T(8,128)S(1)} %get-tuple-element.41), channel_id=1, source_target_pairs={{0,1},{2,3},{4,5},{6,7},{8,9},{10,11},{12,13},{14,15},{16,17},{18,... | collective-permute-start | bytes 36872 | tf_op jit(solution)/shard_map/ppermute | solution.py:379
  63.0 8.2 %collective-permute-start.2 = (f32[24,128]{1,0:T(8,128)S(1)}, f32[24,128]{1,0:T(8,128)S(1)}, u32[]{:S(2)}, u32[]{:S(2)}) collective-permute-start(f32[24,128]{1,0:T(8,128)S(1)} %get-tuple-element.42), channel_id=1, source_target_pairs={{1,2},{3,4},{5,6},{7,8},{9,10},{11,12},{13,14},{15,16},{17,18},{19... | collective-permute-start | bytes 36872 | tf_op jit(solution)/shard_map/ppermute | solution.py:379
  71.9 11.8 %all-to-all-start.4 = ((f32[8,24,128]{2,1,0:T(8,128)}), f32[8,24,128]{2,1,0:T(8,128)S(1)}, u32[]{:S(2)}, u32[]{:S(2)}) async-start(f32[8,24,128]{2,1,0:T(8,128)} %broadcast_in_dim.14), calls=%async_computation.4 | async-start | bytes 196608 | tf_op jit(solution)/shard_map/all_to_all | solution.py:362
  78.7 4.2 %collective-permute-start.3 = (f32[24,128]{1,0:T(8,128)S(1)}, f32[24,128]{1,0:T(8,128)S(1)}, u32[]{:S(2)}, u32[]{:S(2)}) collective-permute-start(f32[24,128]{1,0:T(8,128)S(1)} %get-tuple-element.53), channel_id=1, source_target_pairs={{0,24},{48,72},{96,120},{144,168},{192,216},{240,264},{288,312},{3... | collective-permute-start | bytes 36872 | tf_op jit(solution)/shard_map/ppermute | solution.py:379
